TPU v7x, 128 devices: a whole 4x4x4 slice. The times are simulated.
128 devices in a mesh: wide: 32 (over y, z_lo, x), narrow: 4 (over z_hi, core).
Axes of the slice: x: 4, y: 4, z: 4 (z_hi: 2, z_lo: 2; z = z_hi * 2 + z_lo), core: 2. Of those that a mesh axis runs over, the one named last changes fastest.
Arguments:
- loads: float32 [98304, 512], P('wide', 'narrow'), may hold values from -6 to 6
- start: float32 [98304, 512], P('wide', 'narrow'), may hold values from -6 to 6
- stiffness: bfloat16 [128, 1024, 1024], P('wide')
- local_inverse: bfloat16 [128, 1024, 1024], P('wide')
- modes: bfloat16 [128, 1024, 32], P('wide'), may hold values from -0.1875 to 0.1875
- coarse_inverse: float32 [4096, 4096], P('wide', 'narrow'), as said below
- margin_rows: int32 [128, 256], P('wide'), may hold values from 0 to 98303, as said below
Outputs:
- displacement: float32 [98304, 512], P('wide', 'narrow')
- final_residual: float32 [98304, 512], P('wide', 'narrow')
Inputs may be any that keep to these rules, and one draw needn't show every extreme that they name: Row s lists 256 distinct rows of loads, none of them rows s * 768 to s * 768 + 767. Call rows i * 4 * 768 to (i + 1) * 4 * 768 - 1 block i. For every i, the entries of rows i * 4 to (i + 1) * 4 - 1 of margin_rows fall at most 48 times into any one block, and exactly 48 times into some block. coarse_inverse equals its transpose.
All inputs are finite; a program needn't handle non-finite values.
Results may differ from a plain program's by a relative error of at most 0.0062.
Values may be sent and summed in bfloat16 or wider, within the bound.
A program may use at most 128 MiB of HBM per device.

v0:
```python
import jax
import jax.numpy as jnp
from jax import lax
from jax.sharding import PartitionSpec as P

ITERS = 2


damping = 0.5


def apply_each(matrices, vectors):
    return jnp.einsum("sij,sjc->sic", matrices, vectors, preferred_element_type=jnp.float32)


def shards(loads, start, stiffness, local_inverse, modes, coarse_inverse, margin_rows):
    owners = lax.axis_size("wide")
    sub_count, margin_count = margin_rows.shape
    matrix_order = stiffness.shape[1]
    core_count = matrix_order - margin_count
    held_rows, col_count = loads.shape
    mode_count = modes.shape[2]
    coarse_rows_dev = sub_count * mode_count
    capacity = 3 * sub_count * margin_count // (2 * owners)
    flat_rows = margin_rows.reshape(-1)
    source = flat_rows // held_rows
    remote_row = flat_rows - source * held_rows
    onehot = (source[:, None] == jnp.arange(owners, dtype=jnp.int32)[None, :]).astype(jnp.int32)
    before = jnp.cumsum(onehot, axis=0) - onehot
    placed = source * capacity + jnp.sum(before * onehot, axis=1)
    requested = jnp.full((owners * capacity,), -1, jnp.int32).at[placed].set(remote_row)
    wanted = lax.all_to_all(
        requested.reshape(owners, capacity), "wide", split_axis=0, concat_axis=0, tiled=True
    )
    usable = (wanted >= 0).reshape(-1)
    picked = jnp.where(usable, wanted.reshape(-1), 0)

    def gather_local(field):
        field_low = field.astype(jnp.bfloat16)
        outgoing = jnp.where(usable[:, None], field_low[picked], jnp.zeros((), jnp.bfloat16))
        incoming = lax.all_to_all(
            outgoing.reshape(owners, capacity, col_count),
            "wide",
            split_axis=0,
            concat_axis=0,
            tiled=True,
        )
        outer_part = incoming.reshape(owners * capacity, col_count)[placed].reshape(
            sub_count, margin_count, col_count
        )
        core_part = field_low.reshape(sub_count, core_count, col_count)
        return jnp.concatenate([core_part, outer_part], axis=1)

    def assemble_parts(parts):
        outer_part = parts[:, core_count:, :].reshape(sub_count * margin_count, col_count)
        outgoing = jnp.zeros((owners * capacity, col_count), jnp.float32).at[placed].set(outer_part)
        incoming = lax.all_to_all(
            outgoing.reshape(owners, capacity, col_count),
            "wide",
            split_axis=0,
            concat_axis=0,
            tiled=True,
        )
        summed = parts[:, :core_count, :].reshape(held_rows, col_count)
        return summed.at[picked].add(incoming.reshape(owners * capacity, col_count))

    def residual_of(field):
        return loads - assemble_parts(apply_each(stiffness, gather_local(field)))

    field = start
    for iteration in range(ITERS):
        residual = residual_of(field)
        restricted = gather_local(residual)
        solved_local = apply_each(local_inverse, restricted)
        projection = jnp.einsum(
            "sim,sic->smc", modes, restricted, preferred_element_type=jnp.float32
        )
        solve_projection = projection.reshape(coarse_rows_dev, col_count)
        gathered = lax.all_gather(solve_projection, "wide", axis=0, tiled=True)
        tile_width = coarse_inverse.shape[1]
        row_offset = lax.axis_index("narrow") * tile_width
        selected = lax.dynamic_slice_in_dim(
            lax.all_gather(gathered, "narrow", axis=1, tiled=True), row_offset, tile_width, 0
        )
        partial_sums = jnp.dot(coarse_inverse, selected, precision=lax.Precision.HIGHEST)
        coarse = lax.psum_scatter(partial_sums, "narrow", scatter_dimension=1, tiled=True)
        lifted = jnp.einsum(
            "sim,smc->sic",
            modes.astype(jnp.float32),
            coarse.reshape(sub_count, mode_count, col_count),
            precision=lax.Precision.HIGHEST,
        )
        change = assemble_parts(damping * solved_local + lifted)
        field = field + change
    return (field, residual_of(field))


def solution(mesh):
    placed = (
        P("wide", "narrow"),
        P("wide", "narrow"),
        P("wide", None, None),
        P("wide", None, None),
        P("wide", None, None),
        P("wide", "narrow"),
        P("wide", None),
    )
    return jax.shard_map(
        shards,
        mesh=mesh,
        in_specs=placed,
        out_specs=(P("wide", "narrow"), P("wide", "narrow")),
        check_vma=False,
    )
```

profile of v0, /device:TPU:0, one launch (start us, length us, event | category | flops | bytes accessed | tf_op | source)
XLA Modules:
  0.0 880.0 jit_solution(7259748184903397401)
XLA Ops:
  10.8 9.0 %reduce-window.6 = s32[32,8,128]{2,1,0:T(8,128)S(1)} reduce-window(s32[32,8,128]{2,1,0:T(8,128)S(1)} %fusion.34, s32[]{:T(128)} %constant.15.clone.1), window={size=1x1x128 pad=0_0x0_0x127_0}, to_apply=%region_0.1 | reduce-window | flops 4161536 | bytes 262148 | tf_op jit(solution)/shard_map/reduce-window
  25.4 8.8 all-to-all-start
  35.6 6.7 all-to-all-done
  52.2 9.4 %all-to-all-done.1 = bf16[32,48,128]{2,1,0:T(8,128)(2,1)S(1)} async-done(((bf16[32,48,128]{2,1,0:T(8,128)(2,1)}), bf16[32,48,128]{2,1,0:T(8,128)(2,1)S(1)}, u32[]{:S(2)}, u32[]{:S(2)}) %all-to-all-start.1) | async-done | bytes 393248 | tf_op jit(solution)/shard_map/all_to_all | solution.py:41
  65.6 6.4 convolution_bitcast_fusion.2
  84.6 8.8 %all-to-all-done.2 = f32[32,48,128]{2,1,0:T(8,128)S(1)} async-done(((f32[32,48,128]{2,1,0:T(8,128)}), f32[32,48,128]{2,1,0:T(8,128)S(1)}, u32[]{:S(2)}, u32[]{:S(2)}) %all-to-all-start.2) | async-done | bytes 786464 | tf_op jit(solution)/shard_map/all_to_all | solution.py:57
  93.4 9.4 %scatter_fusion = f32[3072,128]{1,0:T(8,128)S(1)} fusion(f32[3072,128]{1,0:T(8,128)S(1)} %bitcast.119, s32[1536]{0:T(1024)S(1)} %fusion.35, f32[1536,128]{1,0:T(8,128)S(1)} %bitcast.132), kind=kCustom, calls=%fused_computation.12 | custom fusion | flops 196608 | bytes 2365440 | tf_op jit(solution)/shard_map/scatter-add | solution.py:65
  113.5 9.2 %all-to-all-done.3 = bf16[32,48,128]{2,1,0:T(8,128)(2,1)S(1)} async-done(((bf16[32,48,128]{2,1,0:T(8,128)(2,1)}), bf16[32,48,128]{2,1,0:T(8,128)(2,1)S(1)}, u32[]{:S(2)}, u32[]{:S(2)}) %all-to-all-start.3) | async-done | bytes 393248 | tf_op jit(solution)/shard_map/all_to_all | solution.py:41
  127.2 151.5 %all-gather.5.cloned.1.call-done = f32[4096,128]{1,0:T(8,128)} async-done(((f32[128,128]{1,0:T(8,128)}), f32[4096,128]{1,0:T(8,128)}) %all-gather.5.cloned.1.call-update) | async-done | bytes 2097168 | tf_op jit(solution)/shard_map/all_gather | solution.py:79
  278.8 65.2 %all-gather.7.cloned.1.call-done = f32[4096,512]{1,0:T(8,128)} async-done(((f32[4096,128]{1,0:T(8,128)}), f32[4096,512]{1,0:T(8,128)}) %all-gather.7.cloned.1.call-update) | async-done | bytes 8388624 | tf_op jit(solution)/shard_map/all_gather | solution.py:83
  344.0 5.7 fusion.4
  349.7 26.5 %reduce-scatter.3.cloned.1.call-done = f32[128,128]{0,1:T(8,128)} async-done(((f32[128,512]{0,1:T(8,128)}), f32[128,128]{0,1:T(8,128)}) %reduce-scatter.3.cloned.1.call-update) | async-done | bytes 65552 | tf_op jit(solution)/shard_map/reduce_scatter | solution.py:86
  378.2 6.3 add_bitcast_fusion.1
  390.6 7.2 all-to-all-start.4
  399.8 12.1 %all-to-all-done.4 = f32[32,48,128]{2,1,0:T(8,128)S(1)} async-done(((f32[32,48,128]{2,1,0:T(8,128)}), f32[32,48,128]{2,1,0:T(8,128)S(1)}, u32[]{:S(2)}, u32[]{:S(2)}) %all-to-all-start.4) | async-done | bytes 786464 | tf_op jit(solution)/shard_map/all_to_all | solution.py:57
  411.9 9.7 %scatter_fusion.1 = f32[3072,128]{1,0:T(8,128)S(1)} fusion(f32[3072,128]{1,0:T(8,128)S(1)} %bitcast_add_fusion.1, s32[1536]{0:T(1024)S(1)} %fusion.35, f32[1536,128]{1,0:T(8,128)S(1)} %bitcast.135), kind=kCustom, calls=%fused_computation.14 | custom fusion | flops 196608 | bytes 2365440 | tf_op jit(solution)/shard_map/scatter-add | solution.py:65
  432.1 8.5 all-to-all-done.5
  446.4 6.3 convolution_bitcast_fusion.1
  468.1 6.0 all-to-all-done.6
  474.1 10.8 %scatter_fusion.2 = f32[3072,128]{1,0:T(8,128)} fusion(f32[3072,128]{1,0:T(8,128)} %bitcast.120, s32[1536]{0:T(1024)S(1)} %fusion.35, f32[1536,128]{1,0:T(8,128)S(1)} %bitcast.133), kind=kCustom, calls=%fused_computation.16 | custom fusion | flops 196608 | bytes 2365440 | tf_op jit(solution)/shard_map/scatter-add | solution.py:65
  497.4 8.5 all-to-all-done.7
  512.8 149.8 %all-gather.9.cloned.1.call-done = f32[4096,128]{1,0:T(8,128)} async-done(((f32[128,128]{1,0:T(8,128)}), f32[4096,128]{1,0:T(8,128)}) %all-gather.9.cloned.1.call-update) | async-done | bytes 2097168 | tf_op jit(solution)/shard_map/all_gather | solution.py:79
  663.1 64.8 %all-gather.11.cloned.1.call-done = f32[4096,512]{1,0:T(8,128)} async-done(((f32[4096,128]{1,0:T(8,128)}), f32[4096,512]{1,0:T(8,128)}) %all-gather.11.cloned.1.call-update) | async-done | bytes 8388624 | tf_op jit(solution)/shard_map/all_gather | solution.py:83
  733.6 26.4 %reduce-scatter.5.cloned.1.call-done = f32[128,128]{0,1:T(8,128)} async-done(((f32[128,512]{0,1:T(8,128)}), f32[128,128]{0,1:T(8,128)}) %reduce-scatter.5.cloned.1.call-update) | async-done | bytes 65552 | tf_op jit(solution)/shard_map/reduce_scatter | solution.py:86
  762.0 6.3 add_bitcast_fusion
  777.0 7.2 all-to-all-start.8
  786.9 11.5 %all-to-all-done.8 = f32[32,48,128]{2,1,0:T(8,128)S(1)} async-done(((f32[32,48,128]{2,1,0:T(8,128)}), f32[32,48,128]{2,1,0:T(8,128)S(1)}, u32[]{:S(2)}, u32[]{:S(2)}) %all-to-all-start.8) | async-done | bytes 786464 | tf_op jit(solution)/shard_map/all_to_all | solution.py:57
  798.4 10.8 %scatter_fusion.3 = f32[3072,128]{1,0:T(8,128)} fusion(f32[3072,128]{1,0:T(8,128)} %bitcast_add_fusion, s32[1536]{0:T(1024)S(1)} %fusion.35, f32[1536,128]{1,0:T(8,128)S(1)} %bitcast.134), kind=kCustom, calls=%fused_computation.18 | custom fusion | flops 196608 | bytes 2365440 | tf_op jit(solution)/shard_map/scatter-add | solution.py:65
  819.7 9.4 %all-to-all-done.9 = bf16[32,48,128]{2,1,0:T(8,128)(2,1)S(1)} async-done(((bf16[32,48,128]{2,1,0:T(8,128)(2,1)}), bf16[32,48,128]{2,1,0:T(8,128)(2,1)S(1)}, u32[]{:S(2)}, u32[]{:S(2)}) %all-to-all-start.9) | async-done | bytes 393248 | tf_op jit(solution)/shard_map/all_to_all | solution.py:41
  833.1 6.4 convolution_bitcast_fusion
  852.1 8.7 all-to-all-done.10
  860.8 9.4 %scatter_fusion.4 = f32[3072,128]{1,0:T(8,128)S(1)} fusion(f32[3072,128]{1,0:T(8,128)S(1)} %bitcast.118, s32[1536]{0:T(1024)S(1)} %fusion.35, f32[1536,128]{1,0:T(8,128)S(1)} %bitcast.131), kind=kCustom, calls=%fused_computation.20 | custom fusion | flops 196608 | bytes 2365440 | tf_op jit(solution)/shard_map/scatter-add | solution.py:65
  (136 shorter events, 162.4 us)
Async XLA Ops:
  7.2 336.8 %copy-start = (f32[128,1024]{1,0:T(8,128)S(1)}, f32[128,1024]{1,0:T(8,128)}, u32[]{:S(2)}) copy-start(f32[128,1024]{1,0:T(8,128)} %param.12) | copy-start | bytes 1572868
  20.3 52.7 %copy-start.10 = (s32[1024,1]{0,1:T(1,128)}, s32[1024,1]{0,1:T(1,128)S(1)}, u32[]{:S(2)}) copy-start(s32[1024,1]{0,1:T(1,128)S(1)} %compare_select_fusion.2) | copy-start | bytes 12292
  25.4 17.0 %all-to-all-start = ((s32[32,1,48]{2,1,0:T(1,128)}), s32[32,1,48]{2,1,0:T(1,128)S(1)}, u32[]{:S(2)}, u32[]{:S(2)}) async-start(s32[32,1,48]{2,1,0:T(1,128)} %all_to_all.38), calls=%async_computation | async-start | bytes 32768 | tf_op jit(solution)/shard_map/all_to_all | solution.py:32
  42.4 65.2 %copy-start.5 = (pred[32,48]{1,0:T(8,128)(4,1)}, pred[32,48]{1,0:T(8,128)(4,1)S(1)}, u32[]{:S(2)}) copy-start(pred[32,48]{1,0:T(8,128)(4,1)S(1)} %compare_bitcast_fusion) | copy-start | bytes 4612
  48.0 13.6 %all-to-all-start.1 = ((bf16[32,48,128]{2,1,0:T(8,128)(2,1)}), bf16[32,48,128]{2,1,0:T(8,128)(2,1)S(1)}, u32[]{:S(2)}, u32[]{:S(2)}) async-start(bf16[32,48,128]{2,1,0:T(8,128)(2,1)} %broadcast_select_fusion.4), calls=%async_computation.1 | async-start | bytes 786432 | tf_op jit(solution)/shard_map/all_to_all | solution.py:41
  52.1 19.8 %copy-start.7 = (s32[1024]{0:T(1024)}, s32[1024]{0:T(1024)S(1)}, u32[]{:S(2)}) copy-start(s32[1024]{0:T(1024)S(1)} %broadcast_clamp_fusion) | copy-start | bytes 12292
  77.4 16.0 %all-to-all-start.2 = ((f32[32,48,128]{2,1,0:T(8,128)}), f32[32,48,128]{2,1,0:T(8,128)S(1)}, u32[]{:S(2)}, u32[]{:S(2)}) async-start(f32[32,48,128]{2,1,0:T(8,128)} %bitcast.137), calls=%async_computation.2 | async-start | bytes 1572864 | tf_op jit(solution)/shard_map/all_to_all | solution.py:57
  107.6 15.1 %copy-start.8 = (s32[1024]{0:T(1024)S(1)}, s32[1024]{0:T(1024)}, u32[]{:S(2)}) copy-start(s32[1024]{0:T(1024)} %copy-done.7) | copy-start | bytes 12292
  108.6 14.0 %all-to-all-start.3 = ((bf16[32,48,128]{2,1,0:T(8,128)(2,1)}), bf16[32,48,128]{2,1,0:T(8,128)(2,1)S(1)}, u32[]{:S(2)}, u32[]{:S(2)}) async-start(bf16[32,48,128]{2,1,0:T(8,128)(2,1)} %broadcast_select_fusion.3), calls=%async_computation.3 | async-start | bytes 786432 | tf_op jit(solution)/shard_map/all_to_all | solution.py:41
  113.0 165.7 %all-gather.5.cloned.1.call-start = ((), (), s32[]{:S(2)}) async-start(), calls=%async_computation.13 | async-start | bytes 2162688 | tf_op jit(solution)/shard_map/all_gather | solution.py:79
  113.2 12.9 %copy-start.4 = (bf16[4,1024,32]{1,2,0:T(8,128)(2,1)S(1)}, bf16[4,1024,32]{1,2,0:T(8,128)(2,1)}, u32[]{:S(2)}) copy-start(bf16[4,1024,32]{1,2,0:T(8,128)(2,1)} %param.11) | copy-start | bytes 786436
  127.2 216.8 %all-gather.7.cloned.1.call-start = ((), (), s32[]{:S(2)}) async-start(), calls=%async_computation.14 | async-start | bytes 10485760 | tf_op jit(solution)/shard_map/all_gather | solution.py:83
  278.7 97.5 %reduce-scatter.3.cloned.1.call-start = ((), (), s32[]{:S(2)}) async-start(), calls=%async_computation.15 | async-start | bytes 327680 | tf_op jit(solution)/shard_map/reduce_scatter | solution.py:86
  390.6 21.4 %all-to-all-start.4 = ((f32[32,48,128]{2,1,0:T(8,128)}), f32[32,48,128]{2,1,0:T(8,128)S(1)}, u32[]{:S(2)}, u32[]{:S(2)}) async-start(f32[32,48,128]{2,1,0:T(8,128)} %bitcast.26), calls=%async_computation.5 | async-start | bytes 1572864 | tf_op jit(solution)/shard_map/all_to_all | solution.py:57
  426.6 14.0 %all-to-all-start.5 = ((bf16[32,48,128]{2,1,0:T(8,128)(2,1)}), bf16[32,48,128]{2,1,0:T(8,128)(2,1)S(1)}, u32[]{:S(2)}, u32[]{:S(2)}) async-start(bf16[32,48,128]{2,1,0:T(8,128)(2,1)} %broadcast_select_fusion.2), calls=%async_computation.6 | async-start | bytes 786432 | tf_op jit(solution)/shard_map/all_to_all | solution.py:41
  432.1 14.3 %copy-start.2 = (bf16[4,768,128]{1,2,0:T(8,128)(2,1)S(1)}, bf16[4,768,128]{1,2,0:T(8,128)(2,1)}, u32[]{:S(2)}) copy-start(bf16[4,768,128]{1,2,0:T(8,128)(2,1)} %copy.78) | copy-start | bytes 2359300
  452.7 1.3 copy-start.1
  458.3 15.8 %all-to-all-start.6 = ((f32[32,48,128]{2,1,0:T(8,128)}), f32[32,48,128]{2,1,0:T(8,128)S(1)}, u32[]{:S(2)}, u32[]{:S(2)}) async-start(f32[32,48,128]{2,1,0:T(8,128)} %bitcast.138), calls=%async_computation.7 | async-start | bytes 1572864 | tf_op jit(solution)/shard_map/all_to_all | solution.py:57
  491.8 14.1 %all-to-all-start.7 = ((bf16[32,48,128]{2,1,0:T(8,128)(2,1)}), bf16[32,48,128]{2,1,0:T(8,128)(2,1)S(1)}, u32[]{:S(2)}, u32[]{:S(2)}) async-start(bf16[32,48,128]{2,1,0:T(8,128)(2,1)} %broadcast_select_fusion.1), calls=%async_computation.8 | async-start | bytes 786432 | tf_op jit(solution)/shard_map/all_to_all | solution.py:41
  496.2 166.4 %all-gather.9.cloned.1.call-start = ((), (), s32[]{:S(2)}) async-start(), calls=%async_computation.16 | async-start | bytes 2162688 | tf_op jit(solution)/shard_map/all_gather | solution.py:79
  497.4 14.2 %copy-start.3 = (bf16[4,768,128]{1,2,0:T(8,128)(2,1)S(1)}, bf16[4,768,128]{1,2,0:T(8,128)(2,1)}, u32[]{:S(2)}) copy-start(bf16[4,768,128]{1,2,0:T(8,128)(2,1)} %copy.82) | copy-start | bytes 2359300
  512.8 215.1 %all-gather.11.cloned.1.call-start = ((), (), s32[]{:S(2)}) async-start(), calls=%async_computation.17 | async-start | bytes 10485760 | tf_op jit(solution)/shard_map/all_gather | solution.py:83
  662.6 97.4 %reduce-scatter.5.cloned.1.call-start = ((), (), s32[]{:S(2)}) async-start(), calls=%async_computation.18 | async-start | bytes 327680 | tf_op jit(solution)/shard_map/reduce_scatter | solution.py:86
  777.0 21.4 %all-to-all-start.8 = ((f32[32,48,128]{2,1,0:T(8,128)}), f32[32,48,128]{2,1,0:T(8,128)S(1)}, u32[]{:S(2)}, u32[]{:S(2)}) async-start(f32[32,48,128]{2,1,0:T(8,128)} %bitcast.139), calls=%async_computation.10 | async-start | bytes 1572864 | tf_op jit(solution)/shard_map/all_to_all | solution.py:57
  810.6 3.2 copy-start.6
  813.8 15.2 %copy-start.9 = (s32[1024]{0:T(1024)S(1)}, s32[1024]{0:T(1024)}, u32[]{:S(2)}) copy-start(s32[1024]{0:T(1024)} %copy-done.7) | copy-start | bytes 12292
  814.9 14.2 %all-to-all-start.9 = ((bf16[32,48,128]{2,1,0:T(8,128)(2,1)}), bf16[32,48,128]{2,1,0:T(8,128)(2,1)S(1)}, u32[]{:S(2)}, u32[]{:S(2)}) async-start(bf16[32,48,128]{2,1,0:T(8,128)(2,1)} %broadcast_select_fusion), calls=%async_computation.11 | async-start | bytes 786432 | tf_op jit(solution)/shard_map/all_to_all | solution.py:41
  844.9 15.9 %all-to-all-start.10 = ((f32[32,48,128]{2,1,0:T(8,128)}), f32[32,48,128]{2,1,0:T(8,128)S(1)}, u32[]{:S(2)}, u32[]{:S(2)}) async-start(f32[32,48,128]{2,1,0:T(8,128)} %bitcast.136), calls=%async_computation.12 | async-start | bytes 1572864 | tf_op jit(solution)/shard_map/all_to_all | solution.py:57
Sparse Core Ops, SparseCore 0:
  127.3 151.3 all-gather.4
  280.4 63.5 all-gather.6
  349.8 26.2 reduce-scatter.2
  512.9 149.6 all-gather.8
  664.2 63.5 all-gather.10
  733.7 26.2 reduce-scatter.4
where the time goes:
time: 890 us; the launch traced here: 880 us
  waiting for transfers between devices  583 us (66%)
  local copies, waits for them, and re-layouts  93.7 us (11%)
  other arithmetic  83.4 us (9%)
  starting transfers between devices  57.4 us (6%)
  matrix products  47.3 us (5%)
  between operations  14.9 us (2%)
    all_gather x2, waiting for transfers between devices, shards(): gathered = lax.all_gather(solve_projection, 'wide', axis=0, tiled=True)  301 us
    all_gather x2, waiting for transfers between devices, shards(): lax.all_gather(gathered, 'narrow', axis=1, tiled=True)  130 us
    reduce_scatter x2, waiting for transfers between devices, shards(): lax.psum_scatter(partial_sums, 'narrow', scatter_dimension=1, tiled=True)  52.9 us
    scatter-add x5, other arithmetic, assemble_parts(): return summed.at[picked].add(incoming.reshape(owners * capacity, col_count))  50 us
    all_to_all x5, waiting for transfers between devices, assemble_parts(): lax.all_to_all(outgoing.reshape(owners, capacity, col_count), 'wide', spl...  47.1 us
    all_to_all x5, waiting for transfers between devices, gather_local(): lax.all_to_all(outgoing.reshape(owners, capacity, col_count), 'wide', spl...  45.1 us
    dot_general x5, matrix products, apply_each(): jnp.einsum('sij,sjc->sic', matrices, vectors, preferred_element_type=jnp....  31.6 us
    all_to_all x5, starting transfers between devices, assemble_parts(): lax.all_to_all(outgoing.reshape(owners, capacity, col_count), 'wide', spl...  26.4 us
  transfers between devices with their start and end apart: 17, of which 17 were waited for; matrix products, arithmetic and copies ran while one was open for 2% of the time, Pallas kernels for 0%

commit v1 on v0

v1 whole, which is shorter than its diff:
```python
import jax
import jax.numpy as jnp
from jax import lax
from jax.experimental import pallas as pl
from jax.experimental.pallas import tpu as pltpu
from jax.sharding import PartitionSpec as P

MESH = pl.DeviceIdType.MESH
ITERS = 2
SUBS = 4
ORDER = 1024
CORE = 768
MARGIN = ORDER - CORE
COLS = 128
MODES = 32
HELD = SUBS * CORE
OUTER = SUBS * MARGIN
OWNERS = 32
ACROSS = 4
CAP = 48
SLOTS = OWNERS * CAP
COARSE = SUBS * MODES
WIDTH = 1024
STRIP = 128
F32 = jnp.float32
BF16 = jnp.bfloat16
GATHER, SCATTER, REGATHER, CORRECT = 0, 1, 2, 3


def dot(a, b):
    return jnp.dot(a, b, preferred_element_type=F32)


def iota(shape, axis):
    return lax.broadcasted_iota(jnp.int32, shape, axis).astype(F32)


def strip(i):
    return pl.ds(pl.multiple_of(i * STRIP, STRIP), STRIP)


def split_digits(v):
    high = jnp.floor(v * (1.0 / 64.0))
    return high.astype(BF16), (v - high * 64.0).astype(BF16)


def store_column(row, ref):
    same = iota((STRIP, STRIP), 0) == iota((STRIP, STRIP), 1)
    for k in range(row.shape[1] // STRIP):
        piece = jnp.broadcast_to(row[:, k * STRIP:(k + 1) * STRIP], (STRIP, STRIP))
        column = jnp.sum(jnp.where(same, piece, 0.0), axis=1, keepdims=True)
        ref[k * STRIP:(k + 1) * STRIP, :] = jnp.broadcast_to(column, (STRIP, STRIP))


def fill_by_column(out, column):
    rows, width = out.shape

    def body(i, _):
        held = column[strip(i), :]
        lanes = iota((STRIP, STRIP), 1)
        for k in range(width // STRIP):
            out[strip(i), k * STRIP:(k + 1) * STRIP] = jnp.where(held == lanes + float(k * STRIP), 1.0, 0.0).astype(BF16)
        return 0

    lax.fori_loop(0, rows // STRIP, body, 0)


def fill_by_row(out, row):
    rows, width = out.shape

    def body(i, _):
        down = (lax.broadcasted_iota(jnp.int32, (STRIP, STRIP), 0) + i * STRIP).astype(F32)
        for k in range(width // STRIP):
            out[strip(i), k * STRIP:(k + 1) * STRIP] = jnp.where(down == row[:, k * STRIP:(k + 1) * STRIP], 1.0, 0.0).astype(BF16)
        return 0

    lax.fori_loop(0, rows // STRIP, body, 0)


def fill_equal(out, column, row):
    rows, width = out.shape

    def body(i, _):
        held = column[strip(i), :]
        for k in range(width // STRIP):
            out[strip(i), k * STRIP:(k + 1) * STRIP] = jnp.where(held == row[:, k * STRIP:(k + 1) * STRIP], 1.0, 0.0).astype(BF16)
        return 0

    lax.fori_loop(0, rows // STRIP, body, 0)


def kernel(
    loads, start, stiffness, local_inverse, modes, coarse_inverse, margin_rows,
    out_x, out_r,
    k_v, l_v, m_v, mt_v, c_in, c_all, x, base, pair, loc, part, picked,
    pick, pick_t, same, take, take_t, placed_row, wanted_row,
    outer, asked, wanted, send, recv, proj, bring, recv_sem, send_sem, index_sem, proj_sem, coarse_sem,
):
    me = lax.axis_index("wide")
    col = lax.axis_index("narrow")
    barrier = pltpu.get_barrier_semaphore()

    def greet(d, _):
        pl.semaphore_signal(barrier, inc=1, device_id=(lax.rem(me + d, OWNERS), col), device_id_type=MESH)
        return 0

    lax.fori_loop(1, OWNERS, greet, 0)
    for d in range(1, ACROSS):
        pl.semaphore_signal(barrier, inc=1, device_id=(me, lax.rem(col + d, ACROSS)), device_id_type=MESH)

    fetch_start = pltpu.make_async_copy(start, x, bring.at[0])
    fetch_coarse = pltpu.make_async_copy(coarse_inverse, c_in, bring.at[1])
    fetch_stiff = pltpu.make_async_copy(stiffness, k_v, bring.at[2])
    fetch_modes = pltpu.make_async_copy(modes, m_v, bring.at[3])
    fetch_local = pltpu.make_async_copy(local_inverse, l_v, bring.at[4])
    fetch_start.start()
    fetch_coarse.start()
    fetch_stiff.start()
    fetch_modes.start()
    fetch_local.start()

    rows = jnp.concatenate([margin_rows[s:s + 1, :] for s in range(SUBS)], axis=1).astype(F32)
    source = jnp.floor((rows + 0.5) * (1.0 / HELD))
    within = rows - source * HELD
    owned = source == iota((OWNERS, OUTER), 0)
    owned_b = jnp.where(owned, 1.0, 0.0).astype(BF16)

    def earlier(i, _):
        down = (lax.broadcasted_iota(jnp.int32, (STRIP, OUTER), 0) + i * STRIP).astype(F32)
        take[strip(i), :OUTER] = jnp.where(down < iota((STRIP, OUTER), 1), 1.0, 0.0).astype(BF16)
        return 0

    lax.fori_loop(0, OUTER // STRIP, earlier, 0)
    before = dot(owned_b, take[:, :OUTER])
    rank = jnp.sum(jnp.where(owned, before, 0.0), axis=0, keepdims=True)
    placed = source * CAP + rank
    placed_row[...] = placed

    store_column(rank, picked.at[:OUTER])
    ranked = picked[:OUTER, :] == iota((OUTER, STRIP), 1)
    store_column(within + 1.0, picked.at[:OUTER])
    high, low = split_digits(jnp.where(ranked, picked[:OUTER, :], 0.0))
    ask = dot(owned_b, high) * 64.0 + dot(owned_b, low)
    asked[...] = jnp.broadcast_to(ask[:, None, :], (OWNERS, 8, STRIP))

    pl.semaphore_wait(barrier, OWNERS - 1 + ACROSS - 1)

    def ask_owner(d, _):
        peer = lax.rem(me + d, OWNERS)
        pltpu.make_async_remote_copy(
            asked.at[peer], wanted.at[me], index_sem.at[0], index_sem.at[1], device_id=(peer, col), device_id_type=MESH
        ).start()
        return 0

    lax.fori_loop(1, OWNERS, ask_owner, 0)
    wanted[pl.ds(me, 1)] = asked[pl.ds(me, 1)]

    store_column(placed, picked.at[:OUTER])
    fill_by_column(take, picked)
    fill_by_row(take_t, placed_row)

    fetch_coarse.wait()
    c_all[pl.ds(col, 1)] = c_in[...].astype(BF16)[None]
    for d in range(1, ACROSS):
        pltpu.make_async_remote_copy(
            c_all.at[col], c_all.at[col], coarse_sem.at[0], coarse_sem.at[1],
            device_id=(me, lax.rem(col + d, ACROSS)), device_id_type=MESH,
        ).start()

    for k in range(2):
        pltpu.make_async_copy(wanted.at[pl.ds(0, OWNERS - 1)], wanted.at[pl.ds(0, OWNERS - 1)], index_sem.at[k]).wait()
    slot_of = jnp.max(wanted[...], axis=1)
    high, low = split_digits(slot_of)
    slot = iota((STRIP, SLOTS), 1)
    owner_of = jnp.floor((slot + 0.5) * (1.0 / CAP))
    spread = jnp.where(slot - owner_of * CAP == iota((STRIP, SLOTS), 0), 1.0, 0.0).astype(BF16)
    wide = dot(high, spread) * 64.0 + dot(low, spread)
    row = jnp.sum(jnp.where(owner_of[:OWNERS] == iota((OWNERS, SLOTS), 0), wide, 0.0), axis=0, keepdims=True) - 1.0
    wanted_row[...] = row
    store_column(jnp.where(row < 0.0, -2.0, row), picked)
    fill_by_column(pick, picked)

    def ship(which):
        half = which % 2

        def one(d, _):
            peer = lax.rem(me + d, OWNERS)
            pltpu.make_async_remote_copy(
                send.at[half, peer], recv.at[which, me], send_sem.at[which], recv_sem.at[which],
                device_id=(peer, col), device_id_type=MESH,
            ).start()
            return 0

        lax.fori_loop(1, OWNERS, one, 0)
        recv[which, pl.ds(me, 1)] = send[half, pl.ds(me, 1)]

    def arrive(which):
        others = recv.at[which, pl.ds(0, OWNERS - 1)]
        pltpu.make_async_copy(others, others, recv_sem.at[which]).wait()
        pltpu.make_async_copy(others, others, send_sem.at[which]).wait()

    TILE = 384
    EACH = TILE // CAP

    def tile(i):
        return pl.ds(pl.multiple_of(i * TILE, TILE), TILE)

    def put(half, i, value):
        send[half, pl.ds(i * EACH, EACH)] = value.astype(BF16).reshape(EACH, CAP, COLS)

    def received(which):
        return recv[which].reshape(SLOTS, COLS)

    def spread_margin(half):
        def body(i, _):
            put(half, i, dot(take_t[tile(i), :], outer[...]))
            return 0

        lax.fori_loop(0, SLOTS // TILE, body, 0)

    def collect_margin(which):
        def body(s, _):
            block = take[pl.ds(pl.multiple_of(s * MARGIN, MARGIN), MARGIN), :]
            loc[s, CORE:, :] = dot(block, received(which)).astype(BF16)
            return 0

        lax.fori_loop(0, SUBS, body, 0)

    def rows_of(s):
        return pl.ds(pl.multiple_of(s * CORE, CORE), CORE)

    def margin_of(s):
        return pl.ds(pl.multiple_of(s * MARGIN, MARGIN), MARGIN)

    def pick_pairs():
        def split(s, _):
            v = base[rows_of(s), :]
            upper = v.astype(BF16)
            pair[rows_of(s), :COLS] = upper
            pair[rows_of(s), COLS:] = (v - upper.astype(F32)).astype(BF16)
            return 0

        lax.fori_loop(0, SUBS, split, 0)

        def body(i, _):
            both = dot(pick[tile(i), :], pair[...])
            picked[tile(i), :] = both[:, :COLS] + both[:, COLS:]
            return 0

        lax.fori_loop(0, SLOTS // TILE, body, 0)

    def correct_picked(half, which, sign):
        def body(i, _):
            put(half, i, picked[tile(i), :] + sign * dot(same[tile(i), :], received(which)))
            return 0

        lax.fori_loop(0, SLOTS // TILE, body, 0)

    fetch_start.wait()

    def lower(s, _):
        pair[rows_of(s), :COLS] = x[rows_of(s), :].astype(BF16)
        return 0

    lax.fori_loop(0, SUBS, lower, 0)

    def first(i, _):
        put(GATHER % 2, i, dot(pick[tile(i), :], pair[:, :COLS]))
        return 0

    lax.fori_loop(0, SLOTS // TILE, first, 0)
    ship(GATHER)

    fill_equal(same, picked, wanted_row)
    fill_by_row(pick_t, wanted_row)

    fetch_modes.wait()
    unit = jnp.where(iota((MODES, MODES), 0) == iota((MODES, MODES), 1), 1.0, 0.0).astype(BF16)
    for s in range(SUBS):
        mt_v[s] = lax.dot_general(unit, m_v[s], (((1,), (1,)), ((), ())), preferred_element_type=F32).astype(BF16)
    fetch_stiff.wait()

    def iteration(it, _):
        fetch_loads = pltpu.make_async_copy(loads, base, bring.at[5])
        fetch_loads.start()

        def from_core(s, _):
            loc[s, :CORE, :] = x[rows_of(s), :].astype(BF16)
            part[s] = dot(k_v[s, :, :CORE], loc[s, :CORE, :])
            return 0

        lax.fori_loop(0, SUBS, from_core, 0)
        arrive(GATHER)
        collect_margin(GATHER)

        def margin_part(s, _):
            outer[margin_of(s), :] = (part[s, CORE:, :] + dot(k_v[s, CORE:, CORE:], loc[s, CORE:, :])).astype(BF16)
            return 0

        lax.fori_loop(0, SUBS, margin_part, 0)
        spread_margin(SCATTER % 2)
        ship(SCATTER)
        fetch_loads.wait()

        def core_part(s, _):
            base[rows_of(s), :] = base[rows_of(s), :] - (part[s, :CORE, :] + dot(k_v[s, :CORE, CORE:], loc[s, CORE:, :]))
            return 0

        lax.fori_loop(0, SUBS, core_part, 0)

        @pl.when(it < ITERS)
        def _():
            pick_pairs()

        arrive(SCATTER)

        @pl.when(it < ITERS)
        def _():
            correct_picked(REGATHER % 2, SCATTER, -1.0)
            ship(REGATHER)

        def finish_residual(s, _):
            base[rows_of(s), :] = base[rows_of(s), :] - dot(pick_t[rows_of(s), :], received(SCATTER))
            return 0

        lax.fori_loop(0, SUBS, finish_residual, 0)

        @pl.when(it < ITERS)
        def _():
            @pl.when(it == 0)
            def _():
                fetch_local.wait()
                for k in range(2):
                    pltpu.make_async_copy(c_all.at[pl.ds(0, 3)], c_all.at[pl.ds(0, 3)], coarse_sem.at[k]).wait()

            def solve_core(s, _):
                loc[s, :CORE, :] = base[rows_of(s), :].astype(BF16)
                part[s] = dot(l_v[s, :, :CORE], loc[s, :CORE, :])
                return 0

            lax.fori_loop(0, SUBS, solve_core, 0)
            arrive(REGATHER)
            collect_margin(REGATHER)
            projected = [dot(mt_v[s], loc[s]) for s in range(SUBS)]
            proj[pl.ds(me, 1)] = jnp.concatenate(projected, axis=0).astype(BF16)[None]

            def share(d, _):
                pltpu.make_async_remote_copy(
                    proj.at[me], proj.at[me], proj_sem.at[0], proj_sem.at[1],
                    device_id=(lax.rem(me + d, OWNERS), col), device_id_type=MESH,
                ).start()
                return 0

            lax.fori_loop(1, OWNERS, share, 0)

            def solve_margin(s, _):
                whole = part[s] + dot(l_v[s, :, CORE:], loc[s, CORE:, :])
                base[rows_of(s), :] = x[rows_of(s), :] + 0.5 * whole[:CORE]
                part[s, CORE:, :] = 0.5 * whole[CORE:]
                return 0

            lax.fori_loop(0, SUBS, solve_margin, 0)
            for k in range(2):
                pltpu.make_async_copy(
                    proj.at[pl.ds(0, OWNERS - 1)], proj.at[pl.ds(0, OWNERS - 1)], proj_sem.at[k]
                ).wait()
            per = WIDTH // COARSE
            coarse = dot(c_all[0], proj[:per].reshape(WIDTH, COLS))
            for n in range(1, ACROSS):
                coarse = coarse + dot(c_all[n], proj[n * per:(n + 1) * per].reshape(WIDTH, COLS))
            coarse = coarse.astype(BF16)
            for s in range(SUBS):
                mine = coarse[s * MODES:(s + 1) * MODES]
                outer[s * MARGIN:(s + 1) * MARGIN, :] = (part[s, CORE:, :] + dot(m_v[s, CORE:, :], mine)).astype(BF16)
            spread_margin(CORRECT % 2)
            ship(CORRECT)
            for s in range(SUBS):
                mine = coarse[s * MODES:(s + 1) * MODES]
                base[s * CORE:(s + 1) * CORE, :] = base[s * CORE:(s + 1) * CORE, :] + dot(m_v[s, :CORE, :], mine)
            pick_pairs()
            arrive(CORRECT)
            correct_picked(GATHER % 2, CORRECT, 1.0)
            ship(GATHER)

            def finish_step(s, _):
                x[rows_of(s), :] = base[rows_of(s), :] + dot(pick_t[rows_of(s), :], received(CORRECT))
                return 0

            lax.fori_loop(0, SUBS, finish_step, 0)

        return 0

    lax.fori_loop(0, ITERS + 1, iteration, 0)
    give_x = pltpu.make_async_copy(x, out_x, bring.at[6])
    give_r = pltpu.make_async_copy(base, out_r, bring.at[7])
    give_x.start()
    give_r.start()
    give_x.wait()
    give_r.wait()


def shards(loads, start, stiffness, local_inverse, modes, coarse_inverse, margin_rows):
    field = jax.ShapeDtypeStruct((HELD, COLS), F32)
    hbm = pl.BlockSpec(memory_space=pl.ANY)
    return pl.pallas_call(
        kernel,
        out_shape=(field, field),
        in_specs=[hbm] * 6 + [pl.BlockSpec(memory_space=pltpu.VMEM)],
        out_specs=(hbm, hbm),
        scratch_shapes=[
            pltpu.VMEM((SUBS, ORDER, ORDER), BF16),
            pltpu.VMEM((SUBS, ORDER, ORDER), BF16),
            pltpu.VMEM((SUBS, ORDER, MODES), BF16),
            pltpu.VMEM((SUBS, MODES, ORDER), BF16),
            pltpu.VMEM((COARSE, WIDTH), F32),
            pltpu.VMEM((ACROSS, COARSE, WIDTH), BF16),
            pltpu.VMEM((HELD, COLS), F32),
            pltpu.VMEM((HELD, COLS), F32),
            pltpu.VMEM((HELD, 2 * COLS), BF16),
            pltpu.VMEM((SUBS, ORDER, COLS), BF16),
            pltpu.VMEM((SUBS, ORDER, COLS), F32),
            pltpu.VMEM((SLOTS, COLS), F32),
            pltpu.VMEM((SLOTS, HELD), BF16),
            pltpu.VMEM((HELD, SLOTS), BF16),
            pltpu.VMEM((SLOTS, SLOTS), BF16),
            pltpu.VMEM((OUTER, SLOTS), BF16),
            pltpu.VMEM((SLOTS, OUTER), BF16),
            pltpu.VMEM((1, OUTER), F32),
            pltpu.VMEM((1, SLOTS), F32),
            pltpu.VMEM((OUTER, COLS), BF16),
            pltpu.VMEM((OWNERS, 8, STRIP), F32),
            pltpu.VMEM((OWNERS, 8, STRIP), F32),
            pltpu.VMEM((2, OWNERS, CAP, COLS), BF16),
            pltpu.VMEM((4, OWNERS, CAP, COLS), BF16),
            pltpu.VMEM((OWNERS, COARSE, COLS), BF16),
            pltpu.SemaphoreType.DMA((8,)),
            pltpu.SemaphoreType.DMA((4,)),
            pltpu.SemaphoreType.DMA((4,)),
            pltpu.SemaphoreType.DMA((2,)),
            pltpu.SemaphoreType.DMA((2,)),
            pltpu.SemaphoreType.DMA((2,)),
        ],
        compiler_params=pltpu.CompilerParams(
            collective_id=0, has_side_effects=True, vmem_limit_bytes=63 * 1024 * 1024
        ),
    )(loads, start, stiffness, local_inverse, modes, coarse_inverse, margin_rows)


def solution(mesh):
    placed = (
        P("wide", "narrow"),
        P("wide", "narrow"),
        P("wide", None, None),
        P("wide", None, None),
        P("wide", None, None),
        P("wide", "narrow"),
        P("wide", None),
    )
    return jax.shard_map(
        shards,
        mesh=mesh,
        in_specs=placed,
        out_specs=(P("wide", "narrow"), P("wide", "narrow")),
        check_vma=False,
    )
```

time: 890 us -> 148 us (0.17); the launches traced: 880 us -> 148 us
  waiting for transfers between devices: 583 us -> 0 us
  Pallas kernels: 0 us -> 141 us
  local copies, waits for them, and re-layouts: 93.7 us -> 6.18 us
  other arithmetic: 83.4 us -> 0 us
  starting transfers between devices: 57.4 us -> 0 us
  matrix products: 47.3 us -> 0 us
  between operations: 14.9 us -> 0.65 us
    all_gather x4 -> x0, waiting for transfers between devices: 431 us -> none  [the longest x2 301 us: shards(): gathered = lax.all_gather(solve_projection, 'wide', axis=0, tiled=True)]
    pallas_call x0 -> x1, Pallas kernels: none -> 141 us  [shards(): pl.pallas_call(kernel, out_shape=(field, field), in_specs=[hbm] * 6 + [pl...]
    all_to_all x11 -> x0, waiting for transfers between devices: 98.9 us -> none  [the longest x5 47.1 us: assemble_parts(): lax.all_to_all(outgoing.reshape(owners, capacity, col_count), 'wide', spl...]
    all_to_all x11 -> x0, starting transfers between devices: 56.6 us -> none  [the longest x5 26.4 us: assemble_parts(): lax.all_to_all(outgoing.reshape(owners, capacity, col_count), 'wide', spl...]
    reduce_scatter x2 -> x0, waiting for transfers between devices: 52.9 us -> none  [shards(): lax.psum_scatter(partial_sums, 'narrow', scatter_dimension=1, tiled=True)]
    scatter-add x5 -> x0, other arithmetic: 50 us -> none  [assemble_parts(): return summed.at[picked].add(incoming.reshape(owners * capacity, col_count))]
    dot_general x11 -> x0, matrix products: 47.3 us -> none  [the longest x5 31.6 us: apply_each(): jnp.einsum('sij,sjc->sic', matrices, vectors, preferred_element_type=jnp....]
    gather x10 -> x0, local copies, waits for them, and re-layouts: 34.9 us -> none  [the longest x5 18.9 us: gather_local(): incoming.reshape(owners * capacity, col_count)[placed]]
  transfers between devices with their start and end apart: 17 -> 0, of which waited for: 17 -> 0; matrix products, arithmetic and copies ran while one was open for 2% -> 0% of each run, Pallas kernels for 0% -> 0%
where the time goes in v1:
time: 148 us
  Pallas kernels  141 us (95%)
  local copies, waits for them, and re-layouts  6.18 us (4%)
    pallas_call x1, Pallas kernels, shards(): pl.pallas_call(kernel, out_shape=(field, field), in_specs=[hbm] * 6 + [pl...  141 us
    unnamed x5, local copies, waits for them, and re-layouts  6.18 us

profile of v1, /device:TPU:0, one launch (start us, length us, event | category | flops | bytes accessed | tf_op | source)
XLA Modules:
  0.0 148.3 jit_solution(15554569072394923880)
XLA Ops:
  0.6 2.3 %copy.9.modes = bf16[4,1024,32]{2,1,0:T(8,128)(2,1)} copy(bf16[4,1024,32]{1,2,0:T(8,128)(2,1)} %param.11) | data formatting | bytes 524288 | tf_op args[4]
  2.9 141.4 %shard_map.86 = (f32[3072,128]{1,0:T(8,128)}, f32[3072,128]{1,0:T(8,128)}) custom-call(f32[3072,128]{1,0:T(8,128)} %loads.1, f32[3072,128]{1,0:T(8,128)} %start.1, bf16[4,1024,1024]{2,1,0:T(8,128)(2,1)} %stiffness.1, bf16[4,1024,1024]{2,1,0:T(8,128)(2,1)} %local_inverse.1, bf16[4,1024,32]{2,1,0:T(8,128)(2,1)} %copy.9.modes, f32[128,1024]{1,0:T(8,128)} %coarse_inverse.1, ...), custom_call_target="tpu_custom_call" | custom-call | tf_op jit(solution)/shard_map/pallas_call | solution.py:405
  144.3 0.0 copy-start
  144.3 2.8 %copy.12 = f32[3072,128]{1,0:T(8,128)} copy(f32[3072,128]{1,0:T(8,128)} %get-tuple-element.4) | data formatting | bytes 3145728
  147.1 0.0 copy-done
  147.1 1.1 copy.13
Async XLA Ops:
  144.3 2.8 %copy-start = (f32[3072,128]{1,0:T(8,128)S(1)}, f32[3072,128]{1,0:T(8,128)}, u32[]{:S(2)}) copy-start(f32[3072,128]{1,0:T(8,128)} %get-tuple-element.5) | copy-start | bytes 4718596

commit v2 on v1

--- a/solution.py
+++ b/solution.py
@@ -9,6 +9,7 @@
 ITERS = 2
 SUBS = 4
 ORDER = 1024
+TILE = 384
 CORE = 768
 MARGIN = ORDER - CORE
 COLS = 128
@@ -19,12 +20,27 @@
 ACROSS = 4
 CAP = 48
 SLOTS = OWNERS * CAP
+TILES = SLOTS // TILE
+EACH = TILE // CAP
 COARSE = SUBS * MODES
 WIDTH = 1024
 STRIP = 128
 F32 = jnp.float32
 BF16 = jnp.bfloat16
 GATHER, SCATTER, REGATHER, CORRECT = 0, 1, 2, 3
+SIDES = (4, 2, 4)
+
+
+def reach(offset):
+    return sum(min(o, n - o) for o, n in zip(offset, SIDES))
+
+
+OFFSETS = sorted(
+    [(dy, dz, dx) for dy in range(SIDES[0]) for dz in range(SIDES[1]) for dx in range(SIDES[2])],
+    key=reach, reverse=True,
+)
+BACK = [OFFSETS.index(tuple((n - o) % n for o, n in zip(offset, SIDES))) for offset in OFFSETS]
+SELF = OWNERS - 1
 
 
 def dot(a, b):
@@ -90,28 +106,28 @@
 
 
 def kernel(
-    loads, start, stiffness, local_inverse, modes, coarse_inverse, margin_rows,
+    loads, start, stiffness, local_inverse, modes_t, coarse_inverse, margin_rows,
     out_x, out_r,
-    k_v, l_v, m_v, mt_v, c_in, c_all, x, base, pair, loc, part, picked,
-    pick, pick_t, same, take, take_t, placed_row, wanted_row,
+    k_v, l_v, mt_v, c_in, c_all, x, base, pair, loc, part, picked,
+    pick, pick_t, same, take, take_t, slot_modes, slot_modes_t, placed_row, wanted_row,
     outer, asked, wanted, send, recv, proj, bring, recv_sem, send_sem, index_sem, proj_sem, coarse_sem,
 ):
     me = lax.axis_index("wide")
     col = lax.axis_index("narrow")
+    at_y, at_z, at_x = me // 8, lax.rem(me // 4, 2), lax.rem(me, 4)
+    peers = [
+        (lax.rem(at_y + dy, 4) * 2 + lax.rem(at_z + dz, 2)) * 4 + lax.rem(at_x + dx, 4) for dy, dz, dx in OFFSETS
+    ]
     barrier = pltpu.get_barrier_semaphore()
-
-    def greet(d, _):
-        pl.semaphore_signal(barrier, inc=1, device_id=(lax.rem(me + d, OWNERS), col), device_id_type=MESH)
-        return 0
-
-    lax.fori_loop(1, OWNERS, greet, 0)
+    for j in range(SELF):
+        pl.semaphore_signal(barrier, inc=1, device_id=(peers[j], col), device_id_type=MESH)
     for d in range(1, ACROSS):
         pl.semaphore_signal(barrier, inc=1, device_id=(me, lax.rem(col + d, ACROSS)), device_id_type=MESH)
 
     fetch_start = pltpu.make_async_copy(start, x, bring.at[0])
     fetch_coarse = pltpu.make_async_copy(coarse_inverse, c_in, bring.at[1])
     fetch_stiff = pltpu.make_async_copy(stiffness, k_v, bring.at[2])
-    fetch_modes = pltpu.make_async_copy(modes, m_v, bring.at[3])
+    fetch_modes = pltpu.make_async_copy(modes_t, mt_v, bring.at[3])
     fetch_local = pltpu.make_async_copy(local_inverse, l_v, bring.at[4])
     fetch_start.start()
     fetch_coarse.start()
@@ -122,7 +138,11 @@
     rows = jnp.concatenate([margin_rows[s:s + 1, :] for s in range(SUBS)], axis=1).astype(F32)
     source = jnp.floor((rows + 0.5) * (1.0 / HELD))
     within = rows - source * HELD
-    owned = source == iota((OWNERS, OUTER), 0)
+    place = lax.broadcasted_iota(jnp.int32, (OWNERS, OUTER), 0)
+    owner = jnp.zeros((OWNERS, OUTER), jnp.int32)
+    for j in range(OWNERS):
+        owner = jnp.where(place == j, peers[j], owner)
+    owned = source == owner.astype(F32)
     owned_b = jnp.where(owned, 1.0, 0.0).astype(BF16)
 
     def earlier(i, _):
@@ -133,7 +153,7 @@
     lax.fori_loop(0, OUTER // STRIP, earlier, 0)
     before = dot(owned_b, take[:, :OUTER])
     rank = jnp.sum(jnp.where(owned, before, 0.0), axis=0, keepdims=True)
-    placed = source * CAP + rank
+    placed = jnp.sum(jnp.where(owned, before + CAP * place.astype(F32), 0.0), axis=0, keepdims=True)
     placed_row[...] = placed
 
     store_column(rank, picked.at[:OUTER])
@@ -145,27 +165,24 @@
 
     pl.semaphore_wait(barrier, OWNERS - 1 + ACROSS - 1)
 
-    def ask_owner(d, _):
-        peer = lax.rem(me + d, OWNERS)
+    for j in range(SELF):
         pltpu.make_async_remote_copy(
-            asked.at[peer], wanted.at[me], index_sem.at[0], index_sem.at[1], device_id=(peer, col), device_id_type=MESH
+            asked.at[j], wanted.at[BACK[j]], index_sem.at[0], index_sem.at[1],
+            device_id=(peers[j], col), device_id_type=MESH,
         ).start()
-        return 0
-
-    lax.fori_loop(1, OWNERS, ask_owner, 0)
-    wanted[pl.ds(me, 1)] = asked[pl.ds(me, 1)]
+    wanted[SELF] = asked[SELF]
 
     store_column(placed, picked.at[:OUTER])
     fill_by_column(take, picked)
     fill_by_row(take_t, placed_row)
 
-    fetch_coarse.wait()
-    c_all[pl.ds(col, 1)] = c_in[...].astype(BF16)[None]
-    for d in range(1, ACROSS):
-        pltpu.make_async_remote_copy(
-            c_all.at[col], c_all.at[col], coarse_sem.at[0], coarse_sem.at[1],
-            device_id=(me, lax.rem(col + d, ACROSS)), device_id_type=MESH,
-        ).start()
+    fetch_start.wait()
+
+    def lower(s, _):
+        pair[pl.ds(pl.multiple_of(s * CORE, CORE), CORE), :COLS] = x[pl.ds(pl.multiple_of(s * CORE, CORE), CORE), :].astype(BF16)
+        return 0
+
+    lax.fori_loop(0, SUBS, lower, 0)
 
     for k in range(2):
         pltpu.make_async_copy(wanted.at[pl.ds(0, OWNERS - 1)], wanted.at[pl.ds(0, OWNERS - 1)], index_sem.at[k]).wait()
@@ -180,104 +197,88 @@
     store_column(jnp.where(row < 0.0, -2.0, row), picked)
     fill_by_column(pick, picked)
 
-    def ship(which):
+    def ship(which, i):
         half = which % 2
-
-        def one(d, _):
-            peer = lax.rem(me + d, OWNERS)
-            pltpu.make_async_remote_copy(
-                send.at[half, peer], recv.at[which, me], send_sem.at[which], recv_sem.at[which],
-                device_id=(peer, col), device_id_type=MESH,
-            ).start()
-            return 0
-
-        lax.fori_loop(1, OWNERS, one, 0)
-        recv[which, pl.ds(me, 1)] = send[half, pl.ds(me, 1)]
+        for j in range(i * EACH, (i + 1) * EACH):
+            if j == SELF:
+                recv[which, j] = send[half, j]
+            else:
+                pltpu.make_async_remote_copy(
+                    send.at[half, j], recv.at[which, BACK[j]], send_sem.at[which], recv_sem.at[which],
+                    device_id=(peers[j], col), device_id_type=MESH,
+                ).start()
 
     def arrive(which):
         others = recv.at[which, pl.ds(0, OWNERS - 1)]
         pltpu.make_async_copy(others, others, recv_sem.at[which]).wait()
         pltpu.make_async_copy(others, others, send_sem.at[which]).wait()
 
-    TILE = 384
-    EACH = TILE // CAP
-
     def tile(i):
         return pl.ds(pl.multiple_of(i * TILE, TILE), TILE)
 
-    def put(half, i, value):
-        send[half, pl.ds(i * EACH, EACH)] = value.astype(BF16).reshape(EACH, CAP, COLS)
+    def give(which, i, value):
+        send[which % 2, i * EACH:(i + 1) * EACH] = value.astype(BF16).reshape(EACH, CAP, COLS)
+        ship(which, i)
 
     def received(which):
         return recv[which].reshape(SLOTS, COLS)
 
-    def spread_margin(half):
-        def body(i, _):
-            put(half, i, dot(take_t[tile(i), :], outer[...]))
-            return 0
-
-        lax.fori_loop(0, SLOTS // TILE, body, 0)
-
-    def collect_margin(which):
-        def body(s, _):
-            block = take[pl.ds(pl.multiple_of(s * MARGIN, MARGIN), MARGIN), :]
-            loc[s, CORE:, :] = dot(block, received(which)).astype(BF16)
-            return 0
-
-        lax.fori_loop(0, SUBS, body, 0)
-
     def rows_of(s):
         return pl.ds(pl.multiple_of(s * CORE, CORE), CORE)
 
     def margin_of(s):
         return pl.ds(pl.multiple_of(s * MARGIN, MARGIN), MARGIN)
 
+    def halves(v):
+        upper = v.astype(BF16)
+        return upper, (v - upper.astype(F32)).astype(BF16)
+
+    def joined(both):
+        return both[:, :COLS] + both[:, COLS:]
+
     def pick_pairs():
         def split(s, _):
-            v = base[rows_of(s), :]
-            upper = v.astype(BF16)
-            pair[rows_of(s), :COLS] = upper
-            pair[rows_of(s), COLS:] = (v - upper.astype(F32)).astype(BF16)
+            pair[rows_of(s), :COLS], pair[rows_of(s), COLS:] = halves(base[rows_of(s), :])
             return 0
 
         lax.fori_loop(0, SUBS, split, 0)
 
         def body(i, _):
-            both = dot(pick[tile(i), :], pair[...])
-            picked[tile(i), :] = both[:, :COLS] + both[:, COLS:]
+            picked[tile(i), :] = joined(dot(pick[tile(i), :], pair[...]))
             return 0
 
-        lax.fori_loop(0, SLOTS // TILE, body, 0)
-
-    def correct_picked(half, which, sign):
-        def body(i, _):
-            put(half, i, picked[tile(i), :] + sign * dot(same[tile(i), :], received(which)))
-            return 0
-
-        lax.fori_loop(0, SLOTS // TILE, body, 0)
-
-    fetch_start.wait()
-
-    def lower(s, _):
-        pair[rows_of(s), :COLS] = x[rows_of(s), :].astype(BF16)
-        return 0
-
-    lax.fori_loop(0, SUBS, lower, 0)
-
-    def first(i, _):
-        put(GATHER % 2, i, dot(pick[tile(i), :], pair[:, :COLS]))
-        return 0
-
-    lax.fori_loop(0, SLOTS // TILE, first, 0)
-    ship(GATHER)
+        lax.fori_loop(0, TILES, body, 0)
+
+    def correct_picked(to, which, sign):
+        arrived = received(which)
+        for i in range(TILES):
+            give(to, i, picked[i * TILE:(i + 1) * TILE, :] + sign * dot(same[i * TILE:(i + 1) * TILE, :], arrived))
+
+    for i in range(TILES):
+        give(GATHER, i, dot(pick[i * TILE:(i + 1) * TILE, :], pair[:, :COLS]))
+
+    fetch_coarse.wait()
+    c_all[pl.ds(col, 1)] = c_in[...].astype(BF16)[None]
+    for d in range(1, ACROSS):
+        pltpu.make_async_remote_copy(
+            c_all.at[col], c_all.at[col], coarse_sem.at[0], coarse_sem.at[1],
+            device_id=(me, lax.rem(col + d, ACROSS)), device_id_type=MESH,
+        ).start()
 
     fill_equal(same, picked, wanted_row)
     fill_by_row(pick_t, wanted_row)
 
     fetch_modes.wait()
-    unit = jnp.where(iota((MODES, MODES), 0) == iota((MODES, MODES), 1), 1.0, 0.0).astype(BF16)
+    slot_modes_t[:, :OUTER] = jnp.zeros((COARSE, OUTER), BF16)
     for s in range(SUBS):
-        mt_v[s] = lax.dot_general(unit, m_v[s], (((1,), (1,)), ((), ())), preferred_element_type=F32).astype(BF16)
+        slot_modes_t[s * MODES:(s + 1) * MODES, s * MARGIN:(s + 1) * MARGIN] = mt_v[s, :, CORE:]
+    unit = jnp.where(iota((STRIP, STRIP), 0) == iota((STRIP, STRIP), 1), 1.0, 0.0).astype(BF16)
+    for k in range(OUTER // STRIP):
+        outer[k * STRIP:(k + 1) * STRIP, :] = lax.dot_general(
+            unit, slot_modes_t[:, k * STRIP:(k + 1) * STRIP], (((1,), (1,)), ((), ())), preferred_element_type=F32
+        ).astype(BF16)
+    slot_modes[...] = dot(take_t[...], outer[...]).astype(BF16)
+    slot_modes_t[...] = dot(slot_modes_t[:, :OUTER], take[...]).astype(BF16)
     fetch_stiff.wait()
 
     def iteration(it, _):
@@ -291,15 +292,14 @@
 
         lax.fori_loop(0, SUBS, from_core, 0)
         arrive(GATHER)
-        collect_margin(GATHER)
-
-        def margin_part(s, _):
-            outer[margin_of(s), :] = (part[s, CORE:, :] + dot(k_v[s, CORE:, CORE:], loc[s, CORE:, :])).astype(BF16)
-            return 0
-
-        lax.fori_loop(0, SUBS, margin_part, 0)
-        spread_margin(SCATTER % 2)
-        ship(SCATTER)
+        arrived = received(GATHER)
+        for s in range(SUBS):
+            near = slice(s * MARGIN, (s + 1) * MARGIN)
+            margin = dot(take[near, :], arrived).astype(BF16)
+            loc[s, CORE:, :] = margin
+            outer[near, :] = (part[s, CORE:, :] + dot(k_v[s, CORE:, CORE:], margin)).astype(BF16)
+        for i in range(TILES):
+            give(SCATTER, i, dot(take_t[i * TILE:(i + 1) * TILE, :], outer[...]))
         fetch_loads.wait()
 
         def core_part(s, _):
@@ -316,8 +316,7 @@
 
         @pl.when(it < ITERS)
         def _():
-            correct_picked(REGATHER % 2, SCATTER, -1.0)
-            ship(REGATHER)
+            correct_picked(REGATHER, SCATTER, -1.0)
 
         def finish_residual(s, _):
             base[rows_of(s), :] = base[rows_of(s), :] - dot(pick_t[rows_of(s), :], received(SCATTER))
@@ -339,27 +338,29 @@
                 return 0
 
             lax.fori_loop(0, SUBS, solve_core, 0)
+            projected = jnp.concatenate([dot(mt_v[s, :, :CORE], loc[s, :CORE, :]) for s in range(SUBS)], axis=0)
             arrive(REGATHER)
-            collect_margin(REGATHER)
-            projected = [dot(mt_v[s], loc[s]) for s in range(SUBS)]
-            proj[pl.ds(me, 1)] = jnp.concatenate(projected, axis=0).astype(BF16)[None]
-
-            def share(d, _):
+            proj[pl.ds(me, 1)] = (projected + dot(slot_modes_t[...], received(REGATHER))).astype(BF16)[None]
+            for j in range(SELF):
                 pltpu.make_async_remote_copy(
                     proj.at[me], proj.at[me], proj_sem.at[0], proj_sem.at[1],
-                    device_id=(lax.rem(me + d, OWNERS), col), device_id_type=MESH,
+                    device_id=(peers[j], col), device_id_type=MESH,
                 ).start()
+
+            def solve_margin(s, _):
+                margin = dot(take[margin_of(s), :], received(REGATHER)).astype(BF16)
+                whole = part[s] + dot(l_v[s, :, CORE:], margin)
+                base[rows_of(s), :] = x[rows_of(s), :] + 0.5 * whole[:CORE]
+                pair[margin_of(s), :COLS], pair[margin_of(s), COLS:] = halves(0.5 * whole[CORE:])
                 return 0
 
-            lax.fori_loop(1, OWNERS, share, 0)
-
-            def solve_margin(s, _):
-                whole = part[s] + dot(l_v[s, :, CORE:], loc[s, CORE:, :])
-                base[rows_of(s), :] = x[rows_of(s), :] + 0.5 * whole[:CORE]
-                part[s, CORE:, :] = 0.5 * whole[CORE:]
+            lax.fori_loop(0, SUBS, solve_margin, 0)
+
+            def in_slots(i, _):
+                picked[tile(i), :] = joined(dot(take_t[tile(i), :], pair[:OUTER, :]))
                 return 0
 
-            lax.fori_loop(0, SUBS, solve_margin, 0)
+            lax.fori_loop(0, TILES, in_slots, 0)
             for k in range(2):
                 pltpu.make_async_copy(
                     proj.at[pl.ds(0, OWNERS - 1)], proj.at[pl.ds(0, OWNERS - 1)], proj_sem.at[k]
@@ -368,19 +369,19 @@
             coarse = dot(c_all[0], proj[:per].reshape(WIDTH, COLS))
             for n in range(1, ACROSS):
                 coarse = coarse + dot(c_all[n], proj[n * per:(n + 1) * per].reshape(WIDTH, COLS))
-            coarse = coarse.astype(BF16)
+            coarse = jnp.concatenate(halves(coarse), axis=1)
+            for i in range(TILES):
+                lifted = joined(dot(slot_modes[i * TILE:(i + 1) * TILE, :], coarse))
+                give(CORRECT, i, picked[i * TILE:(i + 1) * TILE, :] + lifted)
             for s in range(SUBS):
-                mine = coarse[s * MODES:(s + 1) * MODES]
-                outer[s * MARGIN:(s + 1) * MARGIN, :] = (part[s, CORE:, :] + dot(m_v[s, CORE:, :], mine)).astype(BF16)
-            spread_margin(CORRECT % 2)
-            ship(CORRECT)
-            for s in range(SUBS):
-                mine = coarse[s * MODES:(s + 1) * MODES]
-                base[s * CORE:(s + 1) * CORE, :] = base[s * CORE:(s + 1) * CORE, :] + dot(m_v[s, :CORE, :], mine)
+                lifted = lax.dot_general(
+                    mt_v[s, :, :CORE], coarse[s * MODES:(s + 1) * MODES], (((0,), (0,)), ((), ())),
+                    preferred_element_type=F32,
+                )
+                base[s * CORE:(s + 1) * CORE, :] = base[s * CORE:(s + 1) * CORE, :] + joined(lifted)
             pick_pairs()
             arrive(CORRECT)
-            correct_picked(GATHER % 2, CORRECT, 1.0)
-            ship(GATHER)
+            correct_picked(GATHER, CORRECT, 1.0)
 
             def finish_step(s, _):
                 x[rows_of(s), :] = base[rows_of(s), :] + dot(pick_t[rows_of(s), :], received(CORRECT))
@@ -410,7 +411,6 @@
         scratch_shapes=[
             pltpu.VMEM((SUBS, ORDER, ORDER), BF16),
             pltpu.VMEM((SUBS, ORDER, ORDER), BF16),
-            pltpu.VMEM((SUBS, ORDER, MODES), BF16),
             pltpu.VMEM((SUBS, MODES, ORDER), BF16),
             pltpu.VMEM((COARSE, WIDTH), F32),
             pltpu.VMEM((ACROSS, COARSE, WIDTH), BF16),
@@ -425,6 +425,8 @@
             pltpu.VMEM((SLOTS, SLOTS), BF16),
             pltpu.VMEM((OUTER, SLOTS), BF16),
             pltpu.VMEM((SLOTS, OUTER), BF16),
+            pltpu.VMEM((SLOTS, COARSE), BF16),
+            pltpu.VMEM((COARSE, SLOTS), BF16),
             pltpu.VMEM((1, OUTER), F32),
             pltpu.VMEM((1, SLOTS), F32),
             pltpu.VMEM((OUTER, COLS), BF16),
@@ -443,7 +445,7 @@
         compiler_params=pltpu.CompilerParams(
             collective_id=0, has_side_effects=True, vmem_limit_bytes=63 * 1024 * 1024
         ),
-    )(loads, start, stiffness, local_inverse, modes, coarse_inverse, margin_rows)
+    )(loads, start, stiffness, local_inverse, jnp.swapaxes(modes, 1, 2), coarse_inverse, margin_rows)
 
 
 def solution(mesh):

time: 148 us -> 144 us (0.973)
  local copies, waits for them, and re-layouts: 6.18 us -> 3.92 us
  Pallas kernels: 141 us -> 139 us
    pallas_call x1, Pallas kernels: 141 us -> 139 us  [shards(): pl.pallas_call(kernel, out_shape=(field, field), in_specs=[hbm] * 6 + [pl...]
    unnamed x5 -> x4, local copies, waits for them, and re-layouts: 6.18 us -> 3.92 us
where the time goes in v2:
time: 144 us
  Pallas kernels  139 us (97%)
  local copies, waits for them, and re-layouts  3.92 us (3%)
    pallas_call x1, Pallas kernels, shards(): pl.pallas_call(kernel, out_shape=(field, field), in_specs=[hbm] * 6 + [pl...  139 us
    unnamed x4, local copies, waits for them, and re-layouts  3.92 us

profile of v2, /device:TPU:0, one launch (start us, length us, event | category | flops | bytes accessed | tf_op | source)
XLA Modules:
  0.0 143.6 jit_solution(11554958064782330681)
XLA Ops:
  0.6 139.0 %shard_map.86 = (f32[3072,128]{1,0:T(8,128)}, f32[3072,128]{1,0:T(8,128)}) custom-call(f32[3072,128]{1,0:T(8,128)} %loads.1, f32[3072,128]{1,0:T(8,128)} %start.1, bf16[4,1024,1024]{2,1,0:T(8,128)(2,1)} %stiffness.1, bf16[4,1024,1024]{2,1,0:T(8,128)(2,1)} %local_inverse.1, bf16[4,32,1024]{2,1,0:T(8,128)(2,1)} %bitcast.1, f32[128,1024]{1,0:T(8,128)} %coarse_inverse.1, ...), custom_call_target="tpu_custom_call" | custom-call | tf_op jit(solution)/shard_map/pallas_call | solution.py:406
  139.6 0.0 copy-start
  139.7 2.8 %copy.11 = f32[3072,128]{1,0:T(8,128)} copy(f32[3072,128]{1,0:T(8,128)} %get-tuple-element.4) | data formatting | bytes 3145728
  142.4 0.0 copy-done
  142.4 1.1 copy.12
Async XLA Ops:
  139.6 2.8 %copy-start = (f32[3072,128]{1,0:T(8,128)S(1)}, f32[3072,128]{1,0:T(8,128)}, u32[]{:S(2)}) copy-start(f32[3072,128]{1,0:T(8,128)} %get-tuple-element.5) | copy-start | bytes 4718596

commit v3 on v2

--- a/solution.py
+++ b/solution.py
@@ -68,8 +68,8 @@
         ref[k * STRIP:(k + 1) * STRIP, :] = jnp.broadcast_to(column, (STRIP, STRIP))
 
 
-def fill_by_column(out, column):
-    rows, width = out.shape
+def fill_by_column(out, column, first, last):
+    width = out.shape[1]
 
     def body(i, _):
         held = column[strip(i), :]
@@ -78,7 +78,7 @@
             out[strip(i), k * STRIP:(k + 1) * STRIP] = jnp.where(held == lanes + float(k * STRIP), 1.0, 0.0).astype(BF16)
         return 0
 
-    lax.fori_loop(0, rows // STRIP, body, 0)
+    lax.fori_loop(first, last, body, 0)
 
 
 def fill_by_row(out, row):
@@ -108,9 +108,9 @@
 def kernel(
     loads, start, stiffness, local_inverse, modes_t, coarse_inverse, margin_rows,
     out_x, out_r,
-    k_v, l_v, mt_v, c_in, c_all, x, base, pair, loc, part, picked,
-    pick, pick_t, same, take, take_t, slot_modes, slot_modes_t, placed_row, wanted_row,
-    outer, asked, wanted, send, recv, proj, bring, recv_sem, send_sem, index_sem, proj_sem, coarse_sem,
+    k_v, l_v, mt_v, c_all, x, base, pair, loc, part, picked,
+    pick, pick_t, same, near, take, take_t, slot_modes, slot_modes_t, placed_row, wanted_row,
+    wanted, send, recv, proj, bring, recv_sem, send_sem, index_sem, proj_sem, coarse_sem,
 ):
     me = lax.axis_index("wide")
     col = lax.axis_index("narrow")
@@ -125,12 +125,14 @@
         pl.semaphore_signal(barrier, inc=1, device_id=(me, lax.rem(col + d, ACROSS)), device_id_type=MESH)
 
     fetch_start = pltpu.make_async_copy(start, x, bring.at[0])
-    fetch_coarse = pltpu.make_async_copy(coarse_inverse, c_in, bring.at[1])
     fetch_stiff = pltpu.make_async_copy(stiffness, k_v, bring.at[2])
     fetch_modes = pltpu.make_async_copy(modes_t, mt_v, bring.at[3])
     fetch_local = pltpu.make_async_copy(local_inverse, l_v, bring.at[4])
     fetch_start.start()
-    fetch_coarse.start()
+    for k in range(WIDTH // STRIP):
+        pltpu.make_async_copy(
+            coarse_inverse.at[:, k * STRIP:(k + 1) * STRIP], base.at[k * STRIP:(k + 1) * STRIP], bring.at[1]
+        ).start()
     fetch_stiff.start()
     fetch_modes.start()
     fetch_local.start()
@@ -161,19 +163,19 @@
     store_column(within + 1.0, picked.at[:OUTER])
     high, low = split_digits(jnp.where(ranked, picked[:OUTER, :], 0.0))
     ask = dot(owned_b, high) * 64.0 + dot(owned_b, low)
-    asked[...] = jnp.broadcast_to(ask[:, None, :], (OWNERS, 8, STRIP))
+    part[0, :OWNERS * 8, :] = jnp.broadcast_to(ask[:, None, :], (OWNERS, 8, STRIP)).reshape(OWNERS * 8, STRIP)
 
     pl.semaphore_wait(barrier, OWNERS - 1 + ACROSS - 1)
 
     for j in range(SELF):
         pltpu.make_async_remote_copy(
-            asked.at[j], wanted.at[BACK[j]], index_sem.at[0], index_sem.at[1],
+            part.at[0, j * 8:(j + 1) * 8], wanted.at[BACK[j]], index_sem.at[0], index_sem.at[1],
             device_id=(peers[j], col), device_id_type=MESH,
         ).start()
-    wanted[SELF] = asked[SELF]
+    wanted[SELF] = part[0, SELF * 8:OWNERS * 8, :]
 
     store_column(placed, picked.at[:OUTER])
-    fill_by_column(take, picked)
+    fill_by_column(take, picked, 0, OUTER // STRIP)
     fill_by_row(take_t, placed_row)
 
     fetch_start.wait()
@@ -183,6 +185,18 @@
         return 0
 
     lax.fori_loop(0, SUBS, lower, 0)
+
+    fetch_modes.wait()
+    slot_modes_t[:, :OUTER] = jnp.zeros((COARSE, OUTER), BF16)
+    for s in range(SUBS):
+        slot_modes_t[s * MODES:(s + 1) * MODES, s * MARGIN:(s + 1) * MARGIN] = mt_v[s, :, CORE:]
+    unit = jnp.where(iota((STRIP, STRIP), 0) == iota((STRIP, STRIP), 1), 1.0, 0.0).astype(BF16)
+    for k in range(OUTER // STRIP):
+        pair[k * STRIP:(k + 1) * STRIP, COLS:] = lax.dot_general(
+            unit, slot_modes_t[:, k * STRIP:(k + 1) * STRIP], (((1,), (1,)), ((), ())), preferred_element_type=F32
+        ).astype(BF16)
+    slot_modes[...] = dot(take_t[...], pair[:OUTER, COLS:]).astype(BF16)
+    slot_modes_t[...] = dot(slot_modes_t[:, :OUTER], take[...]).astype(BF16)
 
     for k in range(2):
         pltpu.make_async_copy(wanted.at[pl.ds(0, OWNERS - 1)], wanted.at[pl.ds(0, OWNERS - 1)], index_sem.at[k]).wait()
@@ -195,7 +209,6 @@
     row = jnp.sum(jnp.where(owner_of[:OWNERS] == iota((OWNERS, SLOTS), 0), wide, 0.0), axis=0, keepdims=True) - 1.0
     wanted_row[...] = row
     store_column(jnp.where(row < 0.0, -2.0, row), picked)
-    fill_by_column(pick, picked)
 
     def ship(which, i):
         half = which % 2
@@ -204,14 +217,18 @@
                 recv[which, j] = send[half, j]
             else:
                 pltpu.make_async_remote_copy(
-                    send.at[half, j], recv.at[which, BACK[j]], send_sem.at[which], recv_sem.at[which],
+                    send.at[half, j], recv.at[which, BACK[j]], send_sem.at[which], recv_sem.at[which, BACK[j] // EACH],
                     device_id=(peers[j], col), device_id_type=MESH,
                 ).start()
 
-    def arrive(which):
-        others = recv.at[which, pl.ds(0, OWNERS - 1)]
-        pltpu.make_async_copy(others, others, recv_sem.at[which]).wait()
-        pltpu.make_async_copy(others, others, send_sem.at[which]).wait()
+    def arrive(which, k):
+        first, last = k * EACH, min((k + 1) * EACH, SELF)
+        blocks = recv.at[which, first:last]
+        pltpu.make_async_copy(blocks, blocks, recv_sem.at[which, k]).wait()
+        if k == 0:
+            others = recv.at[which, :SELF]
+            pltpu.make_async_copy(others, others, send_sem.at[which]).wait()
+        return recv[which, k * EACH:(k + 1) * EACH].reshape(TILE, COLS)
 
     def tile(i):
         return pl.ds(pl.multiple_of(i * TILE, TILE), TILE)
@@ -249,16 +266,24 @@
 
         lax.fori_loop(0, TILES, body, 0)
 
-    def correct_picked(to, which, sign):
-        arrived = received(which)
-        for i in range(TILES):
-            give(to, i, picked[i * TILE:(i + 1) * TILE, :] + sign * dot(same[i * TILE:(i + 1) * TILE, :], arrived))
+    def answer(to, which, table, sign):
+        for k in reversed(range(TILES)):
+            arrived = arrive(which, k)
+            for i in range(TILES):
+                rows = slice(i * TILE, (i + 1) * TILE)
+                value = picked[rows, :] + sign * dot(table[rows, k * TILE:(k + 1) * TILE], arrived)
+                if k > 0:
+                    picked[rows, :] = value
+                else:
+                    give(to, i, value)
 
     for i in range(TILES):
+        fill_by_column(pick, picked, i * TILE // STRIP, (i + 1) * TILE // STRIP)
         give(GATHER, i, dot(pick[i * TILE:(i + 1) * TILE, :], pair[:, :COLS]))
 
-    fetch_coarse.wait()
-    c_all[pl.ds(col, 1)] = c_in[...].astype(BF16)[None]
+    pltpu.make_async_copy(base.at[:WIDTH], base.at[:WIDTH], bring.at[1]).wait()
+    for k in range(WIDTH // STRIP):
+        c_all[col, :, k * STRIP:(k + 1) * STRIP] = base[k * STRIP:(k + 1) * STRIP, :].astype(BF16)
     for d in range(1, ACROSS):
         pltpu.make_async_remote_copy(
             c_all.at[col], c_all.at[col], coarse_sem.at[0], coarse_sem.at[1],
@@ -266,20 +291,25 @@
         ).start()
 
     fill_equal(same, picked, wanted_row)
-    fill_by_row(pick_t, wanted_row)
-
-    fetch_modes.wait()
-    slot_modes_t[:, :OUTER] = jnp.zeros((COARSE, OUTER), BF16)
-    for s in range(SUBS):
-        slot_modes_t[s * MODES:(s + 1) * MODES, s * MARGIN:(s + 1) * MARGIN] = mt_v[s, :, CORE:]
-    unit = jnp.where(iota((STRIP, STRIP), 0) == iota((STRIP, STRIP), 1), 1.0, 0.0).astype(BF16)
-    for k in range(OUTER // STRIP):
-        outer[k * STRIP:(k + 1) * STRIP, :] = lax.dot_general(
-            unit, slot_modes_t[:, k * STRIP:(k + 1) * STRIP], (((1,), (1,)), ((), ())), preferred_element_type=F32
-        ).astype(BF16)
-    slot_modes[...] = dot(take_t[...], outer[...]).astype(BF16)
-    slot_modes_t[...] = dot(slot_modes_t[:, :OUTER], take[...]).astype(BF16)
     fetch_stiff.wait()
+
+    def order(c, _):
+        lanes = pl.ds(pl.multiple_of(c * 2 * COLS, 2 * COLS), 2 * COLS)
+        for s in range(SUBS):
+            rows = slice(s * MARGIN, (s + 1) * MARGIN)
+            pair[rows, :] = dot(k_v[s, CORE:, CORE:], take[rows, lanes]).astype(BF16)
+        for i in range(TILES):
+            rows = slice(i * TILE, (i + 1) * TILE)
+            near[rows, lanes] = dot(take_t[rows, :], pair[:OUTER, :]).astype(BF16)
+        return 0
+
+    lax.fori_loop(0, SLOTS // (2 * COLS), order, 0)
+
+    def in_slots(i, _):
+        picked[tile(i), :] = joined(dot(take_t[tile(i), :], pair[:OUTER, :]))
+        return 0
+
+    give_x = pltpu.make_async_copy(x, out_x, bring.at[6])
 
     def iteration(it, _):
         fetch_loads = pltpu.make_async_copy(loads, base, bring.at[5])
@@ -288,22 +318,22 @@
         def from_core(s, _):
             loc[s, :CORE, :] = x[rows_of(s), :].astype(BF16)
             part[s] = dot(k_v[s, :, :CORE], loc[s, :CORE, :])
+            pair[margin_of(s), :COLS], pair[margin_of(s), COLS:] = halves(part[s, CORE:, :])
             return 0
 
         lax.fori_loop(0, SUBS, from_core, 0)
-        arrive(GATHER)
-        arrived = received(GATHER)
-        for s in range(SUBS):
-            near = slice(s * MARGIN, (s + 1) * MARGIN)
-            margin = dot(take[near, :], arrived).astype(BF16)
-            loc[s, CORE:, :] = margin
-            outer[near, :] = (part[s, CORE:, :] + dot(k_v[s, CORE:, CORE:], margin)).astype(BF16)
-        for i in range(TILES):
-            give(SCATTER, i, dot(take_t[i * TILE:(i + 1) * TILE, :], outer[...]))
+        lax.fori_loop(0, TILES, in_slots, 0)
+
+        @pl.when(it == ITERS)
+        def _():
+            give_x.start()
+
+        answer(SCATTER, GATHER, near, 1.0)
         fetch_loads.wait()
 
         def core_part(s, _):
-            base[rows_of(s), :] = base[rows_of(s), :] - (part[s, :CORE, :] + dot(k_v[s, :CORE, CORE:], loc[s, CORE:, :]))
+            margin = dot(take[margin_of(s), :], received(GATHER)).astype(BF16)
+            base[rows_of(s), :] = base[rows_of(s), :] - (part[s, :CORE, :] + dot(k_v[s, :CORE, CORE:], margin))
             return 0
 
         lax.fori_loop(0, SUBS, core_part, 0)
@@ -311,15 +341,24 @@
         @pl.when(it < ITERS)
         def _():
             pick_pairs()
-
-        arrive(SCATTER)
-
-        @pl.when(it < ITERS)
+            answer(REGATHER, SCATTER, same, -1.0)
+
+        @pl.when(it == ITERS)
         def _():
-            correct_picked(REGATHER, SCATTER, -1.0)
+            for k in reversed(range(TILES)):
+                arrive(SCATTER, k)
+
+        @pl.when(it == 0)
+        def _():
+            fill_by_row(pick_t, wanted_row)
 
         def finish_residual(s, _):
             base[rows_of(s), :] = base[rows_of(s), :] - dot(pick_t[rows_of(s), :], received(SCATTER))
+
+            @pl.when(it == ITERS)
+            def _():
+                pltpu.make_async_copy(base.at[rows_of(s)], out_r.at[rows_of(s)], bring.at[7]).start()
+
             return 0
 
         lax.fori_loop(0, SUBS, finish_residual, 0)
@@ -339,8 +378,9 @@
 
             lax.fori_loop(0, SUBS, solve_core, 0)
             projected = jnp.concatenate([dot(mt_v[s, :, :CORE], loc[s, :CORE, :]) for s in range(SUBS)], axis=0)
-            arrive(REGATHER)
-            proj[pl.ds(me, 1)] = (projected + dot(slot_modes_t[...], received(REGATHER))).astype(BF16)[None]
+            for k in reversed(range(TILES)):
+                projected = projected + dot(slot_modes_t[:, k * TILE:(k + 1) * TILE], arrive(REGATHER, k))
+            proj[pl.ds(me, 1)] = projected.astype(BF16)[None]
             for j in range(SELF):
                 pltpu.make_async_remote_copy(
                     proj.at[me], proj.at[me], proj_sem.at[0], proj_sem.at[1],
@@ -355,10 +395,6 @@
                 return 0
 
             lax.fori_loop(0, SUBS, solve_margin, 0)
-
-            def in_slots(i, _):
-                picked[tile(i), :] = joined(dot(take_t[tile(i), :], pair[:OUTER, :]))
-                return 0
 
             lax.fori_loop(0, TILES, in_slots, 0)
             for k in range(2):
@@ -380,8 +416,7 @@
                 )
                 base[s * CORE:(s + 1) * CORE, :] = base[s * CORE:(s + 1) * CORE, :] + joined(lifted)
             pick_pairs()
-            arrive(CORRECT)
-            correct_picked(GATHER, CORRECT, 1.0)
+            answer(GATHER, CORRECT, same, 1.0)
 
             def finish_step(s, _):
                 x[rows_of(s), :] = base[rows_of(s), :] + dot(pick_t[rows_of(s), :], received(CORRECT))
@@ -392,12 +427,8 @@
         return 0
 
     lax.fori_loop(0, ITERS + 1, iteration, 0)
-    give_x = pltpu.make_async_copy(x, out_x, bring.at[6])
-    give_r = pltpu.make_async_copy(base, out_r, bring.at[7])
-    give_x.start()
-    give_r.start()
     give_x.wait()
-    give_r.wait()
+    pltpu.make_async_copy(base, out_r, bring.at[7]).wait()
 
 
 def shards(loads, start, stiffness, local_inverse, modes, coarse_inverse, margin_rows):
@@ -412,7 +443,6 @@
             pltpu.VMEM((SUBS, ORDER, ORDER), BF16),
             pltpu.VMEM((SUBS, ORDER, ORDER), BF16),
             pltpu.VMEM((SUBS, MODES, ORDER), BF16),
-            pltpu.VMEM((COARSE, WIDTH), F32),
             pltpu.VMEM((ACROSS, COARSE, WIDTH), BF16),
             pltpu.VMEM((HELD, COLS), F32),
             pltpu.VMEM((HELD, COLS), F32),
@@ -423,27 +453,26 @@
             pltpu.VMEM((SLOTS, HELD), BF16),
             pltpu.VMEM((HELD, SLOTS), BF16),
             pltpu.VMEM((SLOTS, SLOTS), BF16),
+            pltpu.VMEM((SLOTS, SLOTS), BF16),
             pltpu.VMEM((OUTER, SLOTS), BF16),
             pltpu.VMEM((SLOTS, OUTER), BF16),
             pltpu.VMEM((SLOTS, COARSE), BF16),
             pltpu.VMEM((COARSE, SLOTS), BF16),
             pltpu.VMEM((1, OUTER), F32),
             pltpu.VMEM((1, SLOTS), F32),
-            pltpu.VMEM((OUTER, COLS), BF16),
-            pltpu.VMEM((OWNERS, 8, STRIP), F32),
             pltpu.VMEM((OWNERS, 8, STRIP), F32),
             pltpu.VMEM((2, OWNERS, CAP, COLS), BF16),
             pltpu.VMEM((4, OWNERS, CAP, COLS), BF16),
             pltpu.VMEM((OWNERS, COARSE, COLS), BF16),
             pltpu.SemaphoreType.DMA((8,)),
-            pltpu.SemaphoreType.DMA((4,)),
+            pltpu.SemaphoreType.DMA((4, TILES)),
             pltpu.SemaphoreType.DMA((4,)),
             pltpu.SemaphoreType.DMA((2,)),
             pltpu.SemaphoreType.DMA((2,)),
             pltpu.SemaphoreType.DMA((2,)),
         ],
         compiler_params=pltpu.CompilerParams(
-            collective_id=0, has_side_effects=True, vmem_limit_bytes=63 * 1024 * 1024
+            collective_id=0, has_side_effects=True, vmem_limit_bytes=64 * 1024 * 1024
         ),
     )(loads, start, stiffness, local_inverse, jnp.swapaxes(modes, 1, 2), coarse_inverse, margin_rows)
 

time: 144 us -> 148 us (1.028)
  Pallas kernels: 139 us -> 143 us
    pallas_call x1, Pallas kernels: 139 us -> 143 us  [shards(): pl.pallas_call(kernel, out_shape=(field, field), in_specs=[hbm] * 6 + [pl...]
where the time goes in v3:
time: 148 us
  Pallas kernels  143 us (97%)
  local copies, waits for them, and re-layouts  3.92 us (3%)
    pallas_call x1, Pallas kernels, shards(): pl.pallas_call(kernel, out_shape=(field, field), in_specs=[hbm] * 6 + [pl...  143 us
    unnamed x4, local copies, waits for them, and re-layouts  3.92 us

profile of v3, /device:TPU:0, one launch (start us, length us, event | category | flops | bytes accessed | tf_op | source)
XLA Modules:
  0.0 147.9 jit_solution(11032635121899259177)
XLA Ops:
  0.6 143.3 %shard_map.86 = (f32[3072,128]{1,0:T(8,128)}, f32[3072,128]{1,0:T(8,128)}) custom-call(f32[3072,128]{1,0:T(8,128)} %loads.1, f32[3072,128]{1,0:T(8,128)} %start.1, bf16[4,1024,1024]{2,1,0:T(8,128)(2,1)} %stiffness.1, bf16[4,1024,1024]{2,1,0:T(8,128)(2,1)} %local_inverse.1, bf16[4,32,1024]{2,1,0:T(8,128)(2,1)} %bitcast.1, f32[128,1024]{1,0:T(8,128)} %coarse_inverse.1, ...), custom_call_target="tpu_custom_call" | custom-call | tf_op jit(solution)/shard_map/pallas_call | solution.py:437
  144.0 0.0 copy-start
  144.0 2.8 %copy.11 = f32[3072,128]{1,0:T(8,128)} copy(f32[3072,128]{1,0:T(8,128)} %get-tuple-element.4) | data formatting | bytes 3145728
  146.7 0.0 copy-done
  146.7 1.1 copy.12
Async XLA Ops:
  144.0 2.8 %copy-start = (f32[3072,128]{1,0:T(8,128)S(1)}, f32[3072,128]{1,0:T(8,128)}, u32[]{:S(2)}) copy-start(f32[3072,128]{1,0:T(8,128)} %get-tuple-element.5) | copy-start | bytes 4718596

commit v4 on v2

--- a/solution.py
+++ b/solution.py
@@ -25,6 +25,8 @@
 COARSE = SUBS * MODES
 WIDTH = 1024
 STRIP = 128
+ROWS_Y = 4
+PLANE = 8
 F32 = jnp.float32
 BF16 = jnp.bfloat16
 GATHER, SCATTER, REGATHER, CORRECT = 0, 1, 2, 3
@@ -108,9 +110,9 @@
 def kernel(
     loads, start, stiffness, local_inverse, modes_t, coarse_inverse, margin_rows,
     out_x, out_r,
-    k_v, l_v, mt_v, c_in, c_all, x, base, pair, loc, part, picked,
+    k_v, l_v, mt_v, tile_t, block, x, base, pair, loc, part, picked,
     pick, pick_t, same, take, take_t, slot_modes, slot_modes_t, placed_row, wanted_row,
-    outer, asked, wanted, send, recv, proj, bring, recv_sem, send_sem, index_sem, proj_sem, coarse_sem,
+    outer, asked, wanted, send, recv, proj, bits, sums, bring, recv_sem, send_sem, index_sem, proj_sem, sum_sem, coarse_sem,
 ):
     me = lax.axis_index("wide")
     col = lax.axis_index("narrow")
@@ -121,16 +123,27 @@
     barrier = pltpu.get_barrier_semaphore()
     for j in range(SELF):
         pl.semaphore_signal(barrier, inc=1, device_id=(peers[j], col), device_id_type=MESH)
+    at_q = lax.rem(me, PLANE)
+    stays = col == at_y
+    takers = [(col * PLANE + at_q, lax.rem(col + d, ACROSS)) for d in range(ACROSS)]
     for d in range(1, ACROSS):
-        pl.semaphore_signal(barrier, inc=1, device_id=(me, lax.rem(col + d, ACROSS)), device_id_type=MESH)
+        pl.semaphore_signal(barrier, inc=1, device_id=takers[d], device_id_type=MESH)
+
+    @pl.when(jnp.logical_not(stays))
+    def _():
+        for d in range(1, ROWS_Y):
+            giver = (lax.rem(col + d, ROWS_Y) * PLANE + at_q, at_y)
+            pl.semaphore_signal(barrier, inc=1, device_id=giver, device_id_type=MESH)
 
     fetch_start = pltpu.make_async_copy(start, x, bring.at[0])
-    fetch_coarse = pltpu.make_async_copy(coarse_inverse, c_in, bring.at[1])
     fetch_stiff = pltpu.make_async_copy(stiffness, k_v, bring.at[2])
     fetch_modes = pltpu.make_async_copy(modes_t, mt_v, bring.at[3])
     fetch_local = pltpu.make_async_copy(local_inverse, l_v, bring.at[4])
     fetch_start.start()
-    fetch_coarse.start()
+    for k in range(WIDTH // STRIP):
+        pltpu.make_async_copy(
+            coarse_inverse.at[:, k * STRIP:(k + 1) * STRIP], base.at[k * STRIP:(k + 1) * STRIP], bring.at[1]
+        ).start()
     fetch_stiff.start()
     fetch_modes.start()
     fetch_local.start()
@@ -163,7 +176,7 @@
     ask = dot(owned_b, high) * 64.0 + dot(owned_b, low)
     asked[...] = jnp.broadcast_to(ask[:, None, :], (OWNERS, 8, STRIP))
 
-    pl.semaphore_wait(barrier, OWNERS - 1 + ACROSS - 1)
+    pl.semaphore_wait(barrier, jnp.where(stays, OWNERS - 1 + 3, OWNERS - 1 + 6))
 
     for j in range(SELF):
         pltpu.make_async_remote_copy(
@@ -183,6 +196,18 @@
         return 0
 
     lax.fori_loop(0, SUBS, lower, 0)
+
+    fetch_modes.wait()
+    slot_modes_t[:, :OUTER] = jnp.zeros((COARSE, OUTER), BF16)
+    for s in range(SUBS):
+        slot_modes_t[s * MODES:(s + 1) * MODES, s * MARGIN:(s + 1) * MARGIN] = mt_v[s, :, CORE:]
+    unit = jnp.where(iota((STRIP, STRIP), 0) == iota((STRIP, STRIP), 1), 1.0, 0.0).astype(BF16)
+    for k in range(OUTER // STRIP):
+        outer[k * STRIP:(k + 1) * STRIP, :] = lax.dot_general(
+            unit, slot_modes_t[:, k * STRIP:(k + 1) * STRIP], (((1,), (1,)), ((), ())), preferred_element_type=F32
+        ).astype(BF16)
+    slot_modes[...] = dot(take_t[...], outer[...]).astype(BF16)
+    slot_modes_t[...] = dot(slot_modes_t[:, :OUTER], take[...]).astype(BF16)
 
     for k in range(2):
         pltpu.make_async_copy(wanted.at[pl.ds(0, OWNERS - 1)], wanted.at[pl.ds(0, OWNERS - 1)], index_sem.at[k]).wait()
@@ -197,16 +222,14 @@
     store_column(jnp.where(row < 0.0, -2.0, row), picked)
     fill_by_column(pick, picked)
 
-    def ship(which, i):
+    def ship(which):
         half = which % 2
-        for j in range(i * EACH, (i + 1) * EACH):
-            if j == SELF:
-                recv[which, j] = send[half, j]
-            else:
-                pltpu.make_async_remote_copy(
-                    send.at[half, j], recv.at[which, BACK[j]], send_sem.at[which], recv_sem.at[which],
-                    device_id=(peers[j], col), device_id_type=MESH,
-                ).start()
+        for j in range(SELF):
+            pltpu.make_async_remote_copy(
+                send.at[half, j], recv.at[which, BACK[j]], send_sem.at[which], recv_sem.at[which],
+                device_id=(peers[j], col), device_id_type=MESH,
+            ).start()
+        recv[which, SELF] = send[half, SELF]
 
     def arrive(which):
         others = recv.at[which, pl.ds(0, OWNERS - 1)]
@@ -216,9 +239,8 @@
     def tile(i):
         return pl.ds(pl.multiple_of(i * TILE, TILE), TILE)
 
-    def give(which, i, value):
+    def put(which, i, value):
         send[which % 2, i * EACH:(i + 1) * EACH] = value.astype(BF16).reshape(EACH, CAP, COLS)
-        ship(which, i)
 
     def received(which):
         return recv[which].reshape(SLOTS, COLS)
@@ -252,34 +274,37 @@
     def correct_picked(to, which, sign):
         arrived = received(which)
         for i in range(TILES):
-            give(to, i, picked[i * TILE:(i + 1) * TILE, :] + sign * dot(same[i * TILE:(i + 1) * TILE, :], arrived))
+            put(to, i, picked[i * TILE:(i + 1) * TILE, :] + sign * dot(same[i * TILE:(i + 1) * TILE, :], arrived))
+        ship(to)
 
     for i in range(TILES):
-        give(GATHER, i, dot(pick[i * TILE:(i + 1) * TILE, :], pair[:, :COLS]))
-
-    fetch_coarse.wait()
-    c_all[pl.ds(col, 1)] = c_in[...].astype(BF16)[None]
+        put(GATHER, i, dot(pick[i * TILE:(i + 1) * TILE, :], pair[:, :COLS]))
+    ship(GATHER)
+
+    pltpu.make_async_copy(base.at[:WIDTH], base.at[:WIDTH], bring.at[1]).wait()
+    for k in range(WIDTH // STRIP):
+        tile_t[k * STRIP:(k + 1) * STRIP, :] = base[k * STRIP:(k + 1) * STRIP, :].T.astype(BF16)
+
+    def hand(end):
+        pltpu.make_async_remote_copy(
+            tile_t, block.at[at_y], coarse_sem.at[0], coarse_sem.at[1], device_id=end, device_id_type=MESH
+        ).start()
+
     for d in range(1, ACROSS):
-        pltpu.make_async_remote_copy(
-            c_all.at[col], c_all.at[col], coarse_sem.at[0], coarse_sem.at[1],
-            device_id=(me, lax.rem(col + d, ACROSS)), device_id_type=MESH,
-        ).start()
+        hand(takers[d])
+
+    @pl.when(stays)
+    def _():
+        block[at_y] = tile_t[...]
+
+    @pl.when(jnp.logical_not(stays))
+    def _():
+        hand(takers[0])
 
     fill_equal(same, picked, wanted_row)
-    fill_by_row(pick_t, wanted_row)
-
-    fetch_modes.wait()
-    slot_modes_t[:, :OUTER] = jnp.zeros((COARSE, OUTER), BF16)
-    for s in range(SUBS):
-        slot_modes_t[s * MODES:(s + 1) * MODES, s * MARGIN:(s + 1) * MARGIN] = mt_v[s, :, CORE:]
-    unit = jnp.where(iota((STRIP, STRIP), 0) == iota((STRIP, STRIP), 1), 1.0, 0.0).astype(BF16)
-    for k in range(OUTER // STRIP):
-        outer[k * STRIP:(k + 1) * STRIP, :] = lax.dot_general(
-            unit, slot_modes_t[:, k * STRIP:(k + 1) * STRIP], (((1,), (1,)), ((), ())), preferred_element_type=F32
-        ).astype(BF16)
-    slot_modes[...] = dot(take_t[...], outer[...]).astype(BF16)
-    slot_modes_t[...] = dot(slot_modes_t[:, :OUTER], take[...]).astype(BF16)
     fetch_stiff.wait()
+
+    give_x = pltpu.make_async_copy(x, out_x, bring.at[6])
 
     def iteration(it, _):
         fetch_loads = pltpu.make_async_copy(loads, base, bring.at[5])
@@ -291,6 +316,11 @@
             return 0
 
         lax.fori_loop(0, SUBS, from_core, 0)
+
+        @pl.when(it == ITERS)
+        def _():
+            give_x.start()
+
         arrive(GATHER)
         arrived = received(GATHER)
         for s in range(SUBS):
@@ -299,7 +329,8 @@
             loc[s, CORE:, :] = margin
             outer[near, :] = (part[s, CORE:, :] + dot(k_v[s, CORE:, CORE:], margin)).astype(BF16)
         for i in range(TILES):
-            give(SCATTER, i, dot(take_t[i * TILE:(i + 1) * TILE, :], outer[...]))
+            put(SCATTER, i, dot(take_t[i * TILE:(i + 1) * TILE, :], outer[...]))
+        ship(SCATTER)
         fetch_loads.wait()
 
         def core_part(s, _):
@@ -318,8 +349,17 @@
         def _():
             correct_picked(REGATHER, SCATTER, -1.0)
 
+        @pl.when(it == 0)
+        def _():
+            fill_by_row(pick_t, wanted_row)
+
         def finish_residual(s, _):
             base[rows_of(s), :] = base[rows_of(s), :] - dot(pick_t[rows_of(s), :], received(SCATTER))
+
+            @pl.when(it == ITERS)
+            def _():
+                pltpu.make_async_copy(base.at[rows_of(s)], out_r.at[rows_of(s)], bring.at[7]).start()
+
             return 0
 
         lax.fori_loop(0, SUBS, finish_residual, 0)
@@ -330,7 +370,13 @@
             def _():
                 fetch_local.wait()
                 for k in range(2):
-                    pltpu.make_async_copy(c_all.at[pl.ds(0, 3)], c_all.at[pl.ds(0, 3)], coarse_sem.at[k]).wait()
+                    @pl.when(stays)
+                    def _():
+                        pltpu.make_async_copy(block.at[:3], block.at[:3], coarse_sem.at[k]).wait()
+
+                    @pl.when(jnp.logical_not(stays))
+                    def _():
+                        pltpu.make_async_copy(block, block, coarse_sem.at[k]).wait()
 
             def solve_core(s, _):
                 loc[s, :CORE, :] = base[rows_of(s), :].astype(BF16)
@@ -338,41 +384,62 @@
                 return 0
 
             lax.fori_loop(0, SUBS, solve_core, 0)
+            def finish_margin():
+                def solve(s, _):
+                    margin = dot(take[margin_of(s), :], received(REGATHER)).astype(BF16)
+                    loc[s, CORE:, :] = margin
+                    whole = part[s, CORE:, :] + dot(l_v[s, CORE:, CORE:], margin)
+                    pair[margin_of(s), :COLS], pair[margin_of(s), COLS:] = halves(0.5 * whole)
+                    return 0
+
+                def in_slots(i, _):
+                    picked[tile(i), :] = joined(dot(take_t[tile(i), :], pair[:OUTER, :]))
+                    return 0
+
+                lax.fori_loop(0, SUBS, solve, 0)
+                lax.fori_loop(0, TILES, in_slots, 0)
+
+            def finish_core():
+                def solve(s, _):
+                    whole = part[s, :CORE, :] + dot(l_v[s, :CORE, CORE:], loc[s, CORE:, :])
+                    base[rows_of(s), :] = x[rows_of(s), :] + 0.5 * whole
+                    return 0
+
+                lax.fori_loop(0, SUBS, solve, 0)
+
             projected = jnp.concatenate([dot(mt_v[s, :, :CORE], loc[s, :CORE, :]) for s in range(SUBS)], axis=0)
             arrive(REGATHER)
-            proj[pl.ds(me, 1)] = (projected + dot(slot_modes_t[...], received(REGATHER))).astype(BF16)[None]
-            for j in range(SELF):
+            proj[pl.ds(at_y, 1)] = (projected + dot(slot_modes_t[...], received(REGATHER))).astype(BF16)[None]
+            for dy in (2, 1, 3):
                 pltpu.make_async_remote_copy(
-                    proj.at[me], proj.at[me], proj_sem.at[0], proj_sem.at[1],
-                    device_id=(peers[j], col), device_id_type=MESH,
+                    proj.at[at_y], proj.at[at_y], proj_sem.at[0], proj_sem.at[1],
+                    device_id=(lax.rem(at_y + dy, ROWS_Y) * PLANE + at_q, col), device_id_type=MESH,
                 ).start()
-
-            def solve_margin(s, _):
-                margin = dot(take[margin_of(s), :], received(REGATHER)).astype(BF16)
-                whole = part[s] + dot(l_v[s, :, CORE:], margin)
-                base[rows_of(s), :] = x[rows_of(s), :] + 0.5 * whole[:CORE]
-                pair[margin_of(s), :COLS], pair[margin_of(s), COLS:] = halves(0.5 * whole[CORE:])
-                return 0
-
-            lax.fori_loop(0, SUBS, solve_margin, 0)
-
-            def in_slots(i, _):
-                picked[tile(i), :] = joined(dot(take_t[tile(i), :], pair[:OUTER, :]))
-                return 0
-
-            lax.fori_loop(0, TILES, in_slots, 0)
+            finish_margin()
             for k in range(2):
-                pltpu.make_async_copy(
-                    proj.at[pl.ds(0, OWNERS - 1)], proj.at[pl.ds(0, OWNERS - 1)], proj_sem.at[k]
-                ).wait()
-            per = WIDTH // COARSE
-            coarse = dot(c_all[0], proj[:per].reshape(WIDTH, COLS))
-            for n in range(1, ACROSS):
-                coarse = coarse + dot(c_all[n], proj[n * per:(n + 1) * per].reshape(WIDTH, COLS))
+                pltpu.make_async_copy(proj.at[:3], proj.at[:3], proj_sem.at[k]).wait()
+            total = dot(block[0], proj[0])
+            for k in range(1, ROWS_Y):
+                total = total + dot(block[k], proj[k])
+            bits[...] = total.astype(BF16).reshape(PLANE, COARSE, COLS)
+            for dz, dx in ((1, 2), (0, 2), (1, 1), (1, 3), (1, 0), (0, 1), (0, 3)):
+                there = lax.rem(at_z + dz, 2) * 4 + lax.rem(at_x + dx, 4)
+                pltpu.make_async_remote_copy(
+                    bits.at[there], sums.at[at_q], sum_sem.at[0], sum_sem.at[1],
+                    device_id=(at_y * PLANE + there, col), device_id_type=MESH,
+                ).start()
+            sums[pl.ds(at_q, 1)] = bits[pl.ds(at_q, 1)]
+            finish_core()
+            for k in range(2):
+                pltpu.make_async_copy(sums.at[:PLANE - 1], sums.at[:PLANE - 1], sum_sem.at[k]).wait()
+            coarse = sums[0].astype(F32)
+            for k in range(1, PLANE):
+                coarse = coarse + sums[k].astype(F32)
             coarse = jnp.concatenate(halves(coarse), axis=1)
             for i in range(TILES):
                 lifted = joined(dot(slot_modes[i * TILE:(i + 1) * TILE, :], coarse))
-                give(CORRECT, i, picked[i * TILE:(i + 1) * TILE, :] + lifted)
+                put(CORRECT, i, picked[i * TILE:(i + 1) * TILE, :] + lifted)
+            ship(CORRECT)
             for s in range(SUBS):
                 lifted = lax.dot_general(
                     mt_v[s, :, :CORE], coarse[s * MODES:(s + 1) * MODES], (((0,), (0,)), ((), ())),
@@ -392,12 +459,8 @@
         return 0
 
     lax.fori_loop(0, ITERS + 1, iteration, 0)
-    give_x = pltpu.make_async_copy(x, out_x, bring.at[6])
-    give_r = pltpu.make_async_copy(base, out_r, bring.at[7])
-    give_x.start()
-    give_r.start()
     give_x.wait()
-    give_r.wait()
+    pltpu.make_async_copy(base, out_r, bring.at[7]).wait()
 
 
 def shards(loads, start, stiffness, local_inverse, modes, coarse_inverse, margin_rows):
@@ -412,8 +475,8 @@
             pltpu.VMEM((SUBS, ORDER, ORDER), BF16),
             pltpu.VMEM((SUBS, ORDER, ORDER), BF16),
             pltpu.VMEM((SUBS, MODES, ORDER), BF16),
-            pltpu.VMEM((COARSE, WIDTH), F32),
-            pltpu.VMEM((ACROSS, COARSE, WIDTH), BF16),
+            pltpu.VMEM((WIDTH, COARSE), BF16),
+            pltpu.VMEM((ROWS_Y, WIDTH, COARSE), BF16),
             pltpu.VMEM((HELD, COLS), F32),
             pltpu.VMEM((HELD, COLS), F32),
             pltpu.VMEM((HELD, 2 * COLS), BF16),
@@ -434,10 +497,13 @@
             pltpu.VMEM((OWNERS, 8, STRIP), F32),
             pltpu.VMEM((2, OWNERS, CAP, COLS), BF16),
             pltpu.VMEM((4, OWNERS, CAP, COLS), BF16),
-            pltpu.VMEM((OWNERS, COARSE, COLS), BF16),
+            pltpu.VMEM((ROWS_Y, COARSE, COLS), BF16),
+            pltpu.VMEM((PLANE, COARSE, COLS), BF16),
+            pltpu.VMEM((PLANE, COARSE, COLS), BF16),
             pltpu.SemaphoreType.DMA((8,)),
             pltpu.SemaphoreType.DMA((4,)),
             pltpu.SemaphoreType.DMA((4,)),
+            pltpu.SemaphoreType.DMA((2,)),
             pltpu.SemaphoreType.DMA((2,)),
             pltpu.SemaphoreType.DMA((2,)),
             pltpu.SemaphoreType.DMA((2,)),

time: 144 us -> 148 us (1.028)
  Pallas kernels: 139 us -> 143 us
    pallas_call x1, Pallas kernels: 139 us -> 143 us  [shards(): pl.pallas_call(kernel, out_shape=(field, field), in_specs=[hbm] * 6 + [pl...]
where the time goes in v4:
time: 148 us; the launch traced here: 147 us
  Pallas kernels  143 us (97%)
  local copies, waits for them, and re-layouts  3.92 us (3%)
    pallas_call x1, Pallas kernels, shards(): pl.pallas_call(kernel, out_shape=(field, field), in_specs=[hbm] * 6 + [pl...  143 us
    unnamed x4, local copies, waits for them, and re-layouts  3.92 us

profile of v4, /device:TPU:0, one launch (start us, length us, event | category | flops | bytes accessed | tf_op | source)
XLA Modules:
  0.0 147.4 jit_solution(11805898207535747633)
XLA Ops:
  0.6 142.8 %shard_map.86 = (f32[3072,128]{1,0:T(8,128)}, f32[3072,128]{1,0:T(8,128)}) custom-call(f32[3072,128]{1,0:T(8,128)} %loads.1, f32[3072,128]{1,0:T(8,128)} %start.1, bf16[4,1024,1024]{2,1,0:T(8,128)(2,1)} %stiffness.1, bf16[4,1024,1024]{2,1,0:T(8,128)(2,1)} %local_inverse.1, bf16[4,32,1024]{2,1,0:T(8,128)(2,1)} %bitcast.1, f32[128,1024]{1,0:T(8,128)} %coarse_inverse.1, ...), custom_call_target="tpu_custom_call" | custom-call | tf_op jit(solution)/shard_map/pallas_call | solution.py:469
  143.5 0.0 copy-start
  143.5 2.8 %copy.11 = f32[3072,128]{1,0:T(8,128)} copy(f32[3072,128]{1,0:T(8,128)} %get-tuple-element.4) | data formatting | bytes 3145728
  146.2 0.0 copy-done
  146.2 1.1 copy.12
Async XLA Ops:
  143.5 2.8 %copy-start = (f32[3072,128]{1,0:T(8,128)S(1)}, f32[3072,128]{1,0:T(8,128)}, u32[]{:S(2)}) copy-start(f32[3072,128]{1,0:T(8,128)} %get-tuple-element.5) | copy-start | bytes 4718596

commit v5 on v4

--- a/solution.py
+++ b/solution.py
@@ -112,7 +112,7 @@
     out_x, out_r,
     k_v, l_v, mt_v, tile_t, block, x, base, pair, loc, part, picked,
     pick, pick_t, same, take, take_t, slot_modes, slot_modes_t, placed_row, wanted_row,
-    outer, asked, wanted, send, recv, proj, bits, sums, bring, recv_sem, send_sem, index_sem, proj_sem, sum_sem, coarse_sem,
+    outer, asked, wanted, send, recv, proj, bits, sums, bring, recv_sem, send_sem, index_sem, proj_sem, sum_sem, tile_sem, coarse_sem,
 ):
     me = lax.axis_index("wide")
     col = lax.axis_index("narrow")
@@ -123,17 +123,16 @@
     barrier = pltpu.get_barrier_semaphore()
     for j in range(SELF):
         pl.semaphore_signal(barrier, inc=1, device_id=(peers[j], col), device_id_type=MESH)
+    for d in range(1, ACROSS):
+        pl.semaphore_signal(barrier, inc=1, device_id=(me, lax.rem(col + d, ACROSS)), device_id_type=MESH)
+
     at_q = lax.rem(me, PLANE)
     stays = col == at_y
-    takers = [(col * PLANE + at_q, lax.rem(col + d, ACROSS)) for d in range(ACROSS)]
-    for d in range(1, ACROSS):
-        pl.semaphore_signal(barrier, inc=1, device_id=takers[d], device_id_type=MESH)
+    partner = (col * PLANE + at_q, at_y)
 
     @pl.when(jnp.logical_not(stays))
     def _():
-        for d in range(1, ROWS_Y):
-            giver = (lax.rem(col + d, ROWS_Y) * PLANE + at_q, at_y)
-            pl.semaphore_signal(barrier, inc=1, device_id=giver, device_id_type=MESH)
+        pl.semaphore_signal(barrier, inc=1, device_id=partner, device_id_type=MESH)
 
     fetch_start = pltpu.make_async_copy(start, x, bring.at[0])
     fetch_stiff = pltpu.make_async_copy(stiffness, k_v, bring.at[2])
@@ -176,7 +175,11 @@
     ask = dot(owned_b, high) * 64.0 + dot(owned_b, low)
     asked[...] = jnp.broadcast_to(ask[:, None, :], (OWNERS, 8, STRIP))
 
-    pl.semaphore_wait(barrier, jnp.where(stays, OWNERS - 1 + 3, OWNERS - 1 + 6))
+    pltpu.make_async_copy(base.at[:WIDTH], base.at[:WIDTH], bring.at[1]).wait()
+    for k in range(WIDTH // STRIP):
+        tile_t[k * STRIP:(k + 1) * STRIP, :] = base[k * STRIP:(k + 1) * STRIP, :].T.astype(BF16)
+
+    pl.semaphore_wait(barrier, jnp.where(stays, OWNERS - 1 + 3, OWNERS - 1 + 4))
 
     for j in range(SELF):
         pltpu.make_async_remote_copy(
@@ -184,6 +187,16 @@
             device_id=(peers[j], col), device_id_type=MESH,
         ).start()
     wanted[SELF] = asked[SELF]
+
+    @pl.when(stays)
+    def _():
+        block[col] = tile_t[...]
+
+    @pl.when(jnp.logical_not(stays))
+    def _():
+        pltpu.make_async_remote_copy(
+            tile_t, block.at[at_y], tile_sem.at[0], tile_sem.at[1], device_id=partner, device_id_type=MESH
+        ).start()
 
     store_column(placed, picked.at[:OUTER])
     fill_by_column(take, picked)
@@ -281,25 +294,16 @@
         put(GATHER, i, dot(pick[i * TILE:(i + 1) * TILE, :], pair[:, :COLS]))
     ship(GATHER)
 
-    pltpu.make_async_copy(base.at[:WIDTH], base.at[:WIDTH], bring.at[1]).wait()
-    for k in range(WIDTH // STRIP):
-        tile_t[k * STRIP:(k + 1) * STRIP, :] = base[k * STRIP:(k + 1) * STRIP, :].T.astype(BF16)
-
-    def hand(end):
-        pltpu.make_async_remote_copy(
-            tile_t, block.at[at_y], coarse_sem.at[0], coarse_sem.at[1], device_id=end, device_id_type=MESH
-        ).start()
-
-    for d in range(1, ACROSS):
-        hand(takers[d])
-
-    @pl.when(stays)
-    def _():
-        block[at_y] = tile_t[...]
-
     @pl.when(jnp.logical_not(stays))
     def _():
-        hand(takers[0])
+        for k in range(2):
+            pltpu.make_async_copy(tile_t, tile_t, tile_sem.at[k]).wait()
+
+    for d in range(1, ACROSS):
+        pltpu.make_async_remote_copy(
+            block.at[col], block.at[col], coarse_sem.at[0], coarse_sem.at[1],
+            device_id=(me, lax.rem(col + d, ACROSS)), device_id_type=MESH,
+        ).start()
 
     fill_equal(same, picked, wanted_row)
     fetch_stiff.wait()
@@ -370,13 +374,7 @@
             def _():
                 fetch_local.wait()
                 for k in range(2):
-                    @pl.when(stays)
-                    def _():
-                        pltpu.make_async_copy(block.at[:3], block.at[:3], coarse_sem.at[k]).wait()
-
-                    @pl.when(jnp.logical_not(stays))
-                    def _():
-                        pltpu.make_async_copy(block, block, coarse_sem.at[k]).wait()
+                    pltpu.make_async_copy(block.at[:3], block.at[:3], coarse_sem.at[k]).wait()
 
             def solve_core(s, _):
                 loc[s, :CORE, :] = base[rows_of(s), :].astype(BF16)
@@ -507,6 +505,7 @@
             pltpu.SemaphoreType.DMA((2,)),
             pltpu.SemaphoreType.DMA((2,)),
             pltpu.SemaphoreType.DMA((2,)),
+            pltpu.SemaphoreType.DMA((2,)),
         ],
         compiler_params=pltpu.CompilerParams(
             collective_id=0, has_side_effects=True, vmem_limit_bytes=63 * 1024 * 1024

time: 148 us -> 131 us (0.89)
  Pallas kernels: 143 us -> 127 us
    pallas_call x1, Pallas kernels: 143 us -> 127 us  [shards(): pl.pallas_call(kernel, out_shape=(field, field), in_specs=[hbm] * 6 + [pl...]
where the time goes in v5:
time: 131 us
  Pallas kernels  127 us (97%)
  local copies, waits for them, and re-layouts  3.92 us (3%)
    pallas_call x1, Pallas kernels, shards(): pl.pallas_call(kernel, out_shape=(field, field), in_specs=[hbm] * 6 + [pl...  127 us
    unnamed x4, local copies, waits for them, and re-layouts  3.92 us

profile of v5, /device:TPU:0, one launch (start us, length us, event | category | flops | bytes accessed | tf_op | source)
XLA Modules:
  0.0 131.1 jit_solution(16308680321579331791)
XLA Ops:
  0.6 126.5 %shard_map.86 = (f32[3072,128]{1,0:T(8,128)}, f32[3072,128]{1,0:T(8,128)}) custom-call(f32[3072,128]{1,0:T(8,128)} %loads.1, f32[3072,128]{1,0:T(8,128)} %start.1, bf16[4,1024,1024]{2,1,0:T(8,128)(2,1)} %stiffness.1, bf16[4,1024,1024]{2,1,0:T(8,128)(2,1)} %local_inverse.1, bf16[4,32,1024]{2,1,0:T(8,128)(2,1)} %bitcast.1, f32[128,1024]{1,0:T(8,128)} %coarse_inverse.1, ...), custom_call_target="tpu_custom_call" | custom-call | tf_op jit(solution)/shard_map/pallas_call | solution.py:467
  127.2 0.0 copy-start
  127.2 2.8 %copy.11 = f32[3072,128]{1,0:T(8,128)} copy(f32[3072,128]{1,0:T(8,128)} %get-tuple-element.4) | data formatting | bytes 3145728
  129.9 0.0 copy-done
  129.9 1.1 copy.12
Async XLA Ops:
  127.2 2.8 %copy-start = (f32[3072,128]{1,0:T(8,128)S(1)}, f32[3072,128]{1,0:T(8,128)}, u32[]{:S(2)}) copy-start(f32[3072,128]{1,0:T(8,128)} %get-tuple-element.5) | copy-start | bytes 4718596

commit v6 on v5

--- a/solution.py
+++ b/solution.py
@@ -9,7 +9,7 @@
 ITERS = 2
 SUBS = 4
 ORDER = 1024
-TILE = 384
+TILE = 768
 CORE = 768
 MARGIN = ORDER - CORE
 COLS = 128
@@ -75,9 +75,12 @@
 
     def body(i, _):
         held = column[strip(i), :]
-        lanes = iota((STRIP, STRIP), 1)
+        piece = jnp.floor(held * (1.0 / STRIP))
+        lane = jnp.where(held - piece * STRIP == iota((STRIP, STRIP), 1), 1.0, 0.0).astype(BF16)
+        piece = piece.astype(BF16)
+        nothing = jnp.zeros((STRIP, STRIP), BF16)
         for k in range(width // STRIP):
-            out[strip(i), k * STRIP:(k + 1) * STRIP] = jnp.where(held == lanes + float(k * STRIP), 1.0, 0.0).astype(BF16)
+            out[strip(i), k * STRIP:(k + 1) * STRIP] = jnp.where(piece == jnp.asarray(k, BF16), lane, nothing)
         return 0
 
     lax.fori_loop(0, rows // STRIP, body, 0)

time: 131 us -> 131 us (level)
  no operation moved by 1% of the time
where the time goes in v6:
time: 131 us; the launch traced here: 130 us
  Pallas kernels  126 us (96%)
  local copies, waits for them, and re-layouts  3.92 us (3%)
    pallas_call x1, Pallas kernels, shards(): pl.pallas_call(kernel, out_shape=(field, field), in_specs=[hbm] * 6 + [pl...  126 us
    unnamed x4, local copies, waits for them, and re-layouts  3.92 us

profile of v6, /device:TPU:0, one launch (start us, length us, event | category | flops | bytes accessed | tf_op | source)
XLA Modules:
  0.0 130.1 jit_solution(11221314740179596214)
XLA Ops:
  0.6 125.5 %shard_map.86 = (f32[3072,128]{1,0:T(8,128)}, f32[3072,128]{1,0:T(8,128)}) custom-call(f32[3072,128]{1,0:T(8,128)} %loads.1, f32[3072,128]{1,0:T(8,128)} %start.1, bf16[4,1024,1024]{2,1,0:T(8,128)(2,1)} %stiffness.1, bf16[4,1024,1024]{2,1,0:T(8,128)(2,1)} %local_inverse.1, bf16[4,32,1024]{2,1,0:T(8,128)(2,1)} %bitcast.1, f32[128,1024]{1,0:T(8,128)} %coarse_inverse.1, ...), custom_call_target="tpu_custom_call" | custom-call | tf_op jit(solution)/shard_map/pallas_call | solution.py:470
  126.1 0.0 copy-start
  126.2 2.8 %copy.11 = f32[3072,128]{1,0:T(8,128)} copy(f32[3072,128]{1,0:T(8,128)} %get-tuple-element.4) | data formatting | bytes 3145728
  128.9 0.0 copy-done
  128.9 1.1 copy.12
Async XLA Ops:
  126.1 2.8 %copy-start = (f32[3072,128]{1,0:T(8,128)S(1)}, f32[3072,128]{1,0:T(8,128)}, u32[]{:S(2)}) copy-start(f32[3072,128]{1,0:T(8,128)} %get-tuple-element.5) | copy-start | bytes 4718596
